TPU v7x, 768 devices: a whole 4x8x12 slice. The times are simulated.
768 devices in a mesh: rep: 24 (over z, core), fsdp: 32 (over x, y).
Axes of the slice: x: 4, y: 8, z: 12, core: 2. Of those that a mesh axis runs over, the one named last changes fastest.
Arguments:
- grads: bfloat16 [24, 32, 768, 2048], P('rep', None, 'fsdp'), may hold values from -400 to 400
- momentum: float32 [32, 32, 24, 2048], P('fsdp', None, 'rep'), may hold values from -384 to 384
- owner: int32 [32], replicated, may hold values from 0 to 31, each once
Outputs:
- update: bfloat16 [32, 32, 24, 2048], P(None, 'fsdp', 'rep')
- momentum_out: float32 [32, 32, 24, 2048], P('fsdp', None, 'rep')
Inputs may be any that keep to these rules, and one draw needn't show every extreme that they name: `owner`: every slot holds exactly one expert.
All inputs are finite; a program needn't handle non-finite values.
Results may differ from a plain program's by a relative error of at most 0.012.
Values may be sent and summed in bfloat16 or wider, within the bound.
No kernel may reach another device: no remote copies, remote signals or barrier semaphores. Data moves between devices by JAX's collectives and lax.ppermute only.
A program may use at most 32 MiB of HBM per device.

v0:
```python
import math

import jax
import jax.numpy as jnp
from jax import lax
from jax.sharding import PartitionSpec as P

D = 2048
ITERS = 2


DECAY_RATE = 0.95
NEWTON_A = 3.4445
NEWTON_B = -4.775
NEWTON_C = 2.0315
EPSILON = 1e-07


def finish_rows(own_gram, gram_matrix):
    squared = jnp.dot(own_gram, gram_matrix, preferred_element_type=jnp.float32)
    polynomial = (NEWTON_B * own_gram.astype(jnp.float32) + NEWTON_C * squared).astype(jnp.bfloat16)
    return polynomial


def rows_whole(current, first_row):
    slab_rows = current.shape[0]
    result = current.astype(jnp.float32)
    for iteration in range(ITERS):
        gathered = lax.all_gather(current, "rep", axis=0, tiled=True)
        if iteration == 0:
            values = gathered.astype(jnp.float32)
            frobenius = jnp.sqrt(jnp.sum(values * values))
            whole = (values / (frobenius + EPSILON)).astype(jnp.bfloat16)
            mine = lax.dynamic_slice_in_dim(whole, first_row, slab_rows, 0)
        else:
            whole = gathered
            mine = current
        own_gram = lax.dot_general(
            mine, whole, (((1,), (1,)), ((), ())), preferred_element_type=jnp.float32
        ).astype(jnp.bfloat16)
        gram_matrix = lax.all_gather(own_gram, "rep", axis=0, tiled=True)
        polynomial = finish_rows(own_gram, gram_matrix)
        result = NEWTON_A * mine.astype(jnp.float32) + jnp.dot(
            polynomial, whole, preferred_element_type=jnp.float32
        )
        current = result.astype(jnp.bfloat16)
    return result


def on_device(grads, momentum, owner):
    slots = lax.axis_size("fsdp")
    replica = lax.axis_index("rep")
    width = grads.shape[-1]
    terms = grads[0].astype(jnp.float32)
    summed = lax.psum_scatter(terms, "rep", scatter_dimension=1, tiled=True)
    onehot = (owner[:, None] == jnp.arange(slots, dtype=jnp.int32)[None, :]).astype(jnp.float32)
    outgoing = jnp.einsum("es,eqd->sqd", onehot, summed, precision=lax.Precision.HIGHEST)
    arrived = lax.all_to_all(outgoing, "fsdp", split_axis=0, concat_axis=1, tiled=True)
    grad_rows = arrived[0]
    moment = momentum[0].reshape(-1, width)
    moment_new = DECAY_RATE * moment + grad_rows
    nesterov = (grad_rows + DECAY_RATE * moment_new).astype(jnp.bfloat16)
    slab_rows = nesterov.shape[0]
    first_row = replica * slab_rows
    result = rows_whole(nesterov, first_row)
    factor = math.sqrt(D)
    update_rows = (factor * result).astype(jnp.bfloat16)
    returning = lax.all_to_all(
        update_rows.reshape(slots, slab_rows // slots, width),
        "fsdp",
        split_axis=0,
        concat_axis=0,
        tiled=True,
    )
    updates = jnp.einsum(
        "es,sqd->eqd", onehot.astype(jnp.bfloat16), returning, preferred_element_type=jnp.float32
    ).astype(jnp.bfloat16)
    return (updates[:, None], moment_new.reshape(1, slots, slab_rows // slots, width))


def solution(mesh):
    placed = (P("rep", None, "fsdp", None), P("fsdp", None, "rep", None), P())
    return jax.shard_map(
        on_device,
        mesh=mesh,
        in_specs=placed,
        out_specs=(P(None, "fsdp", "rep", None), P("fsdp", None, "rep", None)),
        check_vma=False,
    )
```

profile of v0, /device:TPU:8, one launch (start us, length us, event | category | flops | bytes accessed | tf_op | source)
XLA Modules:
  0.0 413.9 jit_solution(14185228402014990405)
XLA Ops:
  7.2 0.0 reduce-scatter.2.cloned.1.call-start
  7.2 6.4 %bitcast_convert_fusion = f32[32,24,2048]{2,0,1:T(8,128)} fusion(bf16[1,32,24,2048]{3,2,1,0:T(8,128)(2,1)} %param.3), kind=kLoop, calls=%fused_computation.4 | loop fusion | flops 1572864 | bytes 9437184 | tf_op jit(solution)/shard_map/convert_element_type | solution.py:54
  13.6 0.0 copy-start.3
  13.6 0.0 copy-start.2
  13.6 0.0 reduce-scatter.2.cloned.1.call-update
  13.6 0.0 all-gather.5.cloned.1.call-start
  13.7 103.2 %reduce-scatter.2.cloned.1.call-done = f32[32,1,2048]{2,0,1:T(8,128)} async-done(((f32[32,24,2048]{2,0,1:T(8,128)}), f32[32,1,2048]{2,0,1:T(8,128)}) %reduce-scatter.2.cloned.1.call-update) | async-done | bytes 262160 | tf_op jit(solution)/shard_map/reduce_scatter | solution.py:55
  116.8 0.0 copy-done.3
  116.8 1.3 convolution_bitcast_fusion
  118.1 0.3 copy.13
  118.4 20.7 %all_to_all.14 = f32[32,1,2048]{2,1,0:T(1,128)S(1)} all-to-all(f32[32,1,2048]{2,1,0:T(1,128)S(1)} %copy.13), channel_id=1, replica_groups=mesh['rep'=24,'fsdp'=32] {'fsdp'}, dimensions={0} | all-to-all | bytes 524288 | tf_op jit(solution)/shard_map/all_to_all | solution.py:58
  139.1 0.0 copy-done.2
  139.1 0.8 fusion.12
  140.0 0.0 all-gather.5.cloned.1.call-update
  140.0 0.0 all-gather.7.cloned.1.call-start
  140.1 54.2 %all-gather.5.cloned.1.call-done = bf16[768,2048]{1,0:T(8,128)(2,1)} async-done(((bf16[32,2048]{1,0:T(8,128)(2,1)}), bf16[768,2048]{1,0:T(8,128)(2,1)}) %all-gather.5.cloned.1.call-update) | async-done | bytes 3145744 | tf_op jit(solution)/shard_map/all_gather | solution.py:29
  194.2 4.1 fusion
  199.0 2.6 fusion.1
  201.7 1.7 convolution_convert_fusion.2
  203.3 0.0 all-gather.7.cloned.1.call-update
  203.3 0.0 all-gather.9.cloned.1.call-start
  203.4 56.3 %all-gather.7.cloned.1.call-done = bf16[768,768]{1,0:T(8,128)(2,1)} async-done(((bf16[32,768]{1,0:T(8,128)(2,1)}), bf16[768,768]{1,0:T(8,128)(2,1)}) %all-gather.7.cloned.1.call-update) | async-done | bytes 1179664 | tf_op jit(solution)/shard_map/all_gather | solution.py:41
  259.7 2.8 fusion.3
  262.5 0.0 copy-start.1
  262.6 0.0 all-gather.9.cloned.1.call-update
  262.6 0.0 all-gather.11.cloned.1.call-start
  262.6 57.9 %all-gather.9.cloned.1.call-done = bf16[768,2048]{1,0:T(8,128)(2,1)} async-done(((bf16[32,2048]{1,0:T(8,128)(2,1)}), bf16[768,2048]{1,0:T(8,128)(2,1)}) %all-gather.9.cloned.1.call-update) | async-done | bytes 3145744 | tf_op jit(solution)/shard_map/all_gather | solution.py:29
  320.6 0.0 copy-start
  320.6 3.8 convolution_convert_fusion.1
  324.3 0.0 all-gather.11.cloned.1.call-update
  324.4 56.4 %all-gather.11.cloned.1.call-done = bf16[768,768]{1,0:T(8,128)(2,1)} async-done(((bf16[32,768]{1,0:T(8,128)(2,1)}), bf16[768,768]{1,0:T(8,128)(2,1)}) %all-gather.11.cloned.1.call-update) | async-done | bytes 1179664 | tf_op jit(solution)/shard_map/all_gather | solution.py:41
  380.7 0.0 copy-done.1
  380.7 0.0 copy-done
  380.7 2.8 fusion.6
  383.6 0.5 broadcast.44
  384.1 1.6 reduce
  385.7 0.7 reshape.32
  386.4 9.8 %all-to-all-start.1 = ((bf16[32,2,1024]{2,1,0:T(2,128)(2,1)}), bf16[32,2,1024]{2,1,0:T(2,128)(2,1)S(1)}, u32[]{:S(2)}, u32[]{:S(2)}) async-start(bf16[32,2,1024]{2,1,0:T(2,128)(2,1)} %reshape.32), calls=%async_computation.2 | async-start | bytes 262144 | tf_op jit(solution)/shard_map/all_to_all | solution.py:68
  396.2 1.1 bitcast_add_fusion
  397.4 1.0 copy.16
  398.3 8.0 %all-to-all-done.1 = bf16[32,2,1024]{2,1,0:T(2,128)(2,1)S(1)} async-done(((bf16[32,2,1024]{2,1,0:T(2,128)(2,1)}), bf16[32,2,1024]{2,1,0:T(2,128)(2,1)S(1)}, u32[]{:S(2)}, u32[]{:S(2)}) %all-to-all-start.1) | async-done | bytes 131104 | tf_op jit(solution)/shard_map/all_to_all | solution.py:68
  406.3 0.1 reshape.33
  406.4 0.9 fusion.5
Async XLA Ops:
  7.2 109.6 %reduce-scatter.2.cloned.1.call-start = ((), (), s32[]{:S(2)}) async-start(), calls=%async_computation.3 | async-start | bytes 6553600 | tf_op jit(solution)/shard_map/reduce_scatter | solution.py:55
  13.6 103.2 %copy-start.3 = (s32[32]{0:T(128)S(1)}, s32[32]{0:T(128)}, u32[]{:S(2)}) copy-start(s32[32]{0:T(128)} %param.5) | copy-start | bytes 388
  13.6 125.6 %copy-start.2 = (f32[1,32,1,2048]{3,2,1,0:T(1,128)S(1)}, f32[1,32,1,2048]{3,2,1,0:T(1,128)}, u32[]{:S(2)}) copy-start(f32[1,32,1,2048]{3,2,1,0:T(1,128)} %param.4) | copy-start | bytes 786436
  13.6 180.6 %all-gather.5.cloned.1.call-start = ((), (), s32[]{:S(2)}) async-start(), calls=%async_computation.4 | async-start | bytes 3276800 | tf_op jit(solution)/shard_map/all_gather | solution.py:29
  140.0 119.7 %all-gather.7.cloned.1.call-start = ((), (), s32[]{:S(2)}) async-start(), calls=%async_computation.5 | async-start | bytes 1228800 | tf_op jit(solution)/shard_map/all_gather | solution.py:41
  203.3 117.2 %all-gather.9.cloned.1.call-start = ((), (), s32[]{:S(2)}) async-start(), calls=%async_computation.6 | async-start | bytes 3276800 | tf_op jit(solution)/shard_map/all_gather | solution.py:29
  262.5 118.2 %copy-start.1 = (bf16[32,2048]{1,0:T(8,128)(2,1)S(1)}, bf16[32,2048]{1,0:T(8,128)(2,1)}, u32[]{:S(2)}) copy-start(bf16[32,2048]{1,0:T(8,128)(2,1)} %fusion.3) | copy-start | bytes 393220
  262.6 118.2 %all-gather.11.cloned.1.call-start = ((), (), s32[]{:S(2)}) async-start(), calls=%async_computation.7 | async-start | bytes 1228800 | tf_op jit(solution)/shard_map/all_gather | solution.py:41
  320.6 60.2 %copy-start = (bf16[768,2048]{1,0:T(8,128)(2,1)S(1)}, bf16[768,2048]{1,0:T(8,128)(2,1)}, u32[]{:S(2)}) copy-start(bf16[768,2048]{1,0:T(8,128)(2,1)} %all-gather.9.cloned.1.call-done) | copy-start | bytes 9437188
  386.4 19.9 %all-to-all-start.1 = ((bf16[32,2,1024]{2,1,0:T(2,128)(2,1)}), bf16[32,2,1024]{2,1,0:T(2,128)(2,1)S(1)}, u32[]{:S(2)}, u32[]{:S(2)}) async-start(bf16[32,2,1024]{2,1,0:T(2,128)(2,1)} %reshape.32), calls=%async_computation.2 | async-start | bytes 262144 | tf_op jit(solution)/shard_map/all_to_all | solution.py:68
Sparse Core Ops, SparseCore 0:
  13.7 103.0 reduce-scatter.1
  140.1 54.0 all-gather.4
  203.5 56.2 all-gather.6
  262.7 57.8 all-gather.8
  324.5 56.2 all-gather.10
where the time goes:
time: 414 us
  waiting for transfers between devices  336 us (81%)
  blocking collectives  20.7 us (5%)
  other arithmetic  16.6 us (4%)
  between operations  14.5 us (4%)
  matrix products  13.3 us (3%)
  starting transfers between devices  10.1 us (2%)
    all_gather x2, waiting for transfers between devices, rows_whole(): gram_matrix = lax.all_gather(own_gram, 'rep', axis=0, tiled=True)  113 us
    all_gather x2, waiting for transfers between devices, rows_whole(): gathered = lax.all_gather(current, 'rep', axis=0, tiled=True)  112 us
    reduce_scatter x1, waiting for transfers between devices, on_device(): summed = lax.psum_scatter(terms, 'rep', scatter_dimension=1, tiled=True)  103 us
    all_to_all x1, blocking collectives, on_device(): lax.all_to_all(outgoing, 'fsdp', split_axis=0, concat_axis=1, tiled=True)  20.7 us
    all_to_all x1, starting transfers between devices, on_device(): lax.all_to_all(update_rows.reshape(slots, slab_rows // slots, width), 'fs...  9.85 us
  transfers between devices with their start and end apart: 6, of which 6 were waited for; matrix products, arithmetic and copies ran while one was open for 1% of the time, Pallas kernels for 0%

commit v1 on v0

v1 whole, which is shorter than its diff:
```python
import math

import jax
import jax.numpy as jnp
from jax import lax
from jax.sharding import PartitionSpec as P

DECAY_RATE = 0.95
NEWTON_A = 3.4445
NEWTON_B = -4.775
NEWTON_C = 2.0315
EPSILON = 1e-07

STRIDE = 3

F32 = jnp.float32
BF16 = jnp.bfloat16


def ring(replicas):
    other = [(r, r ^ 1) for r in range(replicas)]
    up = [(r, (r + 2) % replicas) for r in range(replicas)]
    down = [(r, (r - 2) % replicas) for r in range(replicas)]
    return other, up, down


def classes(replicas):
    chips = replicas // 2
    return [
        [2 * z + core for z in range(first, chips, STRIDE)]
        for first in range(STRIDE)
        for core in range(2)
    ]


def pick(array, index, axis):
    return lax.dynamic_index_in_dim(array, index, axis, keepdims=False)


def sum_rows(grads, replica, replicas):
    experts, _, width = grads.shape
    other, up, down = ring(replicas)
    core = replica % 2
    kind = (replica // 2) % STRIDE
    rows = grads.transpose(1, 0, 2).reshape(replicas // (2 * STRIDE), STRIDE, 2, experts, width)
    mine = pick(rows, core, 2)
    theirs = lax.ppermute(pick(rows, 1 - core, 2), "rep", other)

    def chip_sum(which):
        return pick(mine, which, 1).astype(F32) + pick(theirs, which, 1).astype(F32)

    from_below = lax.ppermute(chip_sum((kind + 1) % STRIDE).astype(BF16), "rep", up)
    from_above = lax.ppermute(chip_sum((kind + 2) % STRIDE).astype(BF16), "rep", down)
    cluster = (chip_sum(kind) + from_below.astype(F32) + from_above.astype(F32)).astype(BF16)
    return lax.all_to_all(cluster, "rep", 0, 0, tiled=True, axis_index_groups=classes(replicas))


def gather_rows(rows, replicas):
    other, up, down = ring(replicas)
    own = lax.all_gather(rows, "rep", axis=0, tiled=True, axis_index_groups=classes(replicas))
    below = lax.ppermute(own, "rep", up)
    above = lax.ppermute(own, "rep", down)
    pieces = [own, below, above]
    return jnp.concatenate(pieces + [lax.ppermute(piece, "rep", other) for piece in pieces], axis=0)


def newton_rows(whole, rows, first_row):
    count = rows.shape[0]
    raw = lax.dot_general(whole, whole, (((1,), (1,)), ((), ())), preferred_element_type=F32)
    size = raw.shape[0]
    diagonal = lax.broadcasted_iota(jnp.int32, (size, size), 0) == lax.broadcasted_iota(jnp.int32, (size, size), 1)
    scale = 1.0 / (jnp.sqrt(jnp.sum(jnp.where(diagonal, raw, 0.0))) + EPSILON)
    gram = (raw * scale * scale).astype(BF16)

    def dot(a, b):
        return jnp.dot(a, b, preferred_element_type=F32)

    def own(matrix):
        return lax.dynamic_slice_in_dim(matrix, first_row, count, 0)

    poly = (NEWTON_B * gram.astype(F32) + NEWTON_C * dot(gram, gram)).astype(BF16)
    mixed = dot(gram, poly).astype(BF16)
    gram_next = (
        NEWTON_A * NEWTON_A * gram.astype(F32) + 2.0 * NEWTON_A * mixed.astype(F32) + dot(mixed, poly)
    ).astype(BF16)
    own_gram = own(gram_next)
    own_poly = (NEWTON_B * own_gram.astype(F32) + NEWTON_C * dot(own_gram, gram_next)).astype(BF16)
    weights = NEWTON_A * (own(poly).astype(F32) + own_poly.astype(F32)) + dot(own_poly, poly)
    return scale * (NEWTON_A * NEWTON_A * rows.astype(F32) + dot(weights.astype(BF16), whole))


def on_device(grads, momentum, owner):
    slots = lax.axis_size("fsdp")
    replicas = lax.axis_size("rep")
    replica = lax.axis_index("rep")
    width = grads.shape[-1]
    lanes = math.gcd(width, 128)
    tiled = (slots, width // lanes, lanes)

    terms = sum_rows(grads[0], replica, replicas)
    onehot = (owner[None, :] == jnp.arange(slots, dtype=jnp.int32)[:, None]).astype(BF16)
    every = jnp.concatenate([onehot] * terms.shape[0], axis=1)
    outgoing = jnp.dot(every, terms.reshape(-1, width), preferred_element_type=F32)
    grad_rows = lax.all_to_all(outgoing.reshape(tiled), "fsdp", split_axis=0, concat_axis=0, tiled=True)
    moment_new = DECAY_RATE * momentum.reshape(tiled) + grad_rows
    nesterov = (grad_rows + DECAY_RATE * moment_new).astype(BF16).reshape(slots, width)

    whole = gather_rows(nesterov, replicas)
    result = newton_rows(whole, nesterov, (replica // (2 * STRIDE)) * slots)
    update_rows = (math.sqrt(width) * result).astype(BF16)

    returning = lax.all_to_all(update_rows.reshape(tiled), "fsdp", split_axis=0, concat_axis=0, tiled=True)
    updates = jnp.einsum(
        "se,sd->ed", onehot, returning.reshape(slots, width), preferred_element_type=F32
    ).astype(BF16)
    return (updates[:, None, None], moment_new.reshape(momentum.shape))


def solution(mesh):
    placed = (P("rep", None, "fsdp", None), P("fsdp", None, "rep", None), P())
    return jax.shard_map(
        on_device,
        mesh=mesh,
        in_specs=placed,
        out_specs=(P(None, "fsdp", "rep", None), P("fsdp", None, "rep", None)),
        check_vma=False,
    )
```

time: 414 us -> 169 us (0.41)
  waiting for transfers between devices: 336 us -> 51.9 us
  starting transfers between devices: 10.1 us -> 48.9 us
  blocking collectives: 20.7 us -> 36.4 us
  between operations: 14.5 us -> 1.72 us
  other arithmetic: 16.6 us -> 7.96 us
  local copies, waits for them, and re-layouts: 2.6 us -> 9.41 us
    all_gather x4 -> x0, waiting for transfers between devices: 225 us -> none  [the longest x2 113 us: rows_whole(): gram_matrix = lax.all_gather(own_gram, 'rep', axis=0, tiled=True)]
    reduce_scatter x1 -> x0, waiting for transfers between devices: 103 us -> none  [on_device(): summed = lax.psum_scatter(terms, 'rep', scatter_dimension=1, tiled=True)]
    ppermute x0 -> x8, starting transfers between devices: none -> 32.5 us  [the longest x1 12.2 us: sum_rows(): lax.ppermute(chip_sum((kind + 2) % STRIDE).astype(BF16), 'rep', down)]
    all_to_all x1 -> x2, waiting for transfers between devices: 7.99 us -> 32.2 us  [the longest x1 21.5 us: sum_rows(): lax.all_to_all(cluster, 'rep', 0, 0, tiled=True, axis_index_groups=classe...]
    all_gather x0 -> x1, blocking collectives: none -> 21 us  [gather_rows(): lax.all_gather(rows, 'rep', axis=0, tiled=True, axis_index_groups=classes...]
    ppermute x0 -> x8, waiting for transfers between devices: none -> 19.7 us  [the longest x1 10.6 us: sum_rows(): lax.ppermute(chip_sum((kind + 1) % STRIDE).astype(BF16), 'rep', up)]
    all_to_all x1 -> x2, starting transfers between devices: 9.85 us -> 16.4 us  [the longest x1 10.2 us: on_device(): lax.all_to_all(outgoing.reshape(tiled), 'fsdp', split_axis=0, concat_axis...]
    all_to_all x1, blocking collectives: 20.7 us -> 15.4 us  [on_device(): lax.all_to_all(update_rows.reshape(tiled), 'fsdp', split_axis=0, concat_a...]
  transfers between devices with their start and end apart: 6 -> 10, of which waited for: 6 -> 8; matrix products, arithmetic and copies ran while one was open for 1% -> 2% of each run, Pallas kernels for 0% -> 0%
where the time goes in v1:
time: 169 us; the launch traced here: 168 us
  waiting for transfers between devices  51.9 us (31%)
  starting transfers between devices  48.9 us (29%)
  blocking collectives  36.4 us (22%)
  matrix products  11.7 us (7%)
  local copies, waits for them, and re-layouts  9.41 us (6%)
  other arithmetic  7.96 us (5%)
  between operations  1.72 us (1%)
    all_to_all x1, waiting for transfers between devices, sum_rows(): lax.all_to_all(cluster, 'rep', 0, 0, tiled=True, axis_index_groups=classe...  21.5 us
    all_gather x1, blocking collectives, gather_rows(): lax.all_gather(rows, 'rep', axis=0, tiled=True, axis_index_groups=classes...  21 us
    all_to_all x1, blocking collectives, on_device(): lax.all_to_all(update_rows.reshape(tiled), 'fsdp', split_axis=0, concat_a...  15.4 us
    ppermute x1, starting transfers between devices, sum_rows(): lax.ppermute(chip_sum((kind + 2) % STRIDE).astype(BF16), 'rep', down)  12.2 us
    all_to_all x1, waiting for transfers between devices, on_device(): lax.all_to_all(outgoing.reshape(tiled), 'fsdp', split_axis=0, concat_axis...  10.7 us
    ppermute x1, waiting for transfers between devices, sum_rows(): lax.ppermute(chip_sum((kind + 1) % STRIDE).astype(BF16), 'rep', up)  10.6 us
    all_to_all x1, starting transfers between devices, on_device(): lax.all_to_all(outgoing.reshape(tiled), 'fsdp', split_axis=0, concat_axis...  10.2 us
    unnamed x14, local copies, waits for them, and re-layouts  6.99 us
  transfers between devices with their start and end apart: 10, of which 8 were waited for; matrix products, arithmetic and copies ran while one was open for 2% of the time, Pallas kernels for 0%

profile of v1, /device:TPU:8, one launch (start us, length us, event | category | flops | bytes accessed | tf_op | source)
XLA Modules:
  0.0 168.0 jit_solution(11785012593819491282)
XLA Ops:
  0.6 3.6 %copy.23 = bf16[1,32,24,2048]{3,1,2,0:T(8,128)(2,1)S(1)} copy(bf16[1,32,24,2048]{3,2,1,0:T(8,128)(2,1)} %param.3) | data formatting | bytes 6291456 | tf_op args[0]
  4.3 1.2 copy_bitcast_fusion
  5.5 1.9 %collective-permute-start = (bf16[4,3,32,2048]{3,2,0,1:T(8,128)(2,1)}, bf16[4,3,32,2048]{3,2,0,1:T(8,128)(2,1)}, u32[]{:S(2)}, u32[]{:S(2)}) collective-permute-start(bf16[4,3,32,2048]{3,2,0,1:T(8,128)(2,1)} %copy_bitcast_fusion), channel_id=1, source_target_pairs={{0,32},{32,0},{64,96},{96,64},{128,160},{160,128},{192,224},{224,1... | collective-permute-start | bytes 4718600 | tf_op jit(solution)/shard_map/ppermute | solution.py:47
  7.5 3.6 %collective-permute-done = bf16[4,3,32,2048]{3,2,0,1:T(8,128)(2,1)} collective-permute-done((bf16[4,3,32,2048]{3,2,0,1:T(8,128)(2,1)}, bf16[4,3,32,2048]{3,2,0,1:T(8,128)(2,1)}, u32[]{:S(2)}, u32[]{:S(2)}) %collective-permute-start) | collective-permute-done | bytes 1572896 | tf_op jit(solution)/shard_map/ppermute | solution.py:47
  11.2 2.6 %fusion.14 = (bf16[4,32,2048]{2,1,0:T(8,128)(2,1)}, bf16[4,32,2048]{2,1,0:T(8,128)(2,1)}) fusion(bf16[4,3,32,2048]{3,2,0,1:T(8,128)(2,1)} %collective-permute-done, s32[]{:T(128)S(6)} %select_n.71, bf16[4,3,2,32,2048]{4,3,2,1,0:T(8,128)(2,1)S(1)} %bitcast.67, s32[]{:T(128)S(6)} %select_n.72, s32[]{:T(128)S(6)} %select_n.68, s32[]{:T(128)S(6)} %select_n.74, ...), kind=kLoop, calls=%fused_computation.27 | loop fusion | flops 2097152 | bytes 3145748 | tf_op jit(solution)/shard_map/convert_element_type | solution.py:52
  13.7 0.0 copy-start.2
  13.7 4.4 %collective-permute-start.1 = (bf16[4,32,2048]{2,1,0:T(8,128)(2,1)}, bf16[4,32,2048]{2,1,0:T(8,128)(2,1)}, u32[]{:S(2)}, u32[]{:S(2)}) collective-permute-start(bf16[4,32,2048]{2,1,0:T(8,128)(2,1)} %get-tuple-element.10), channel_id=1, source_target_pairs={{0,64},{32,96},{64,128},{96,160},{128,192},{160,224},{192,256},{22... | collective-permute-start | bytes 1572872 | tf_op jit(solution)/shard_map/ppermute | solution.py:52
  18.1 12.2 %collective-permute-start.2 = (bf16[4,32,2048]{2,1,0:T(8,128)(2,1)}, bf16[4,32,2048]{2,1,0:T(8,128)(2,1)}, u32[]{:S(2)}, u32[]{:S(2)}) collective-permute-start(bf16[4,32,2048]{2,1,0:T(8,128)(2,1)} %get-tuple-element.11), channel_id=1, source_target_pairs={{0,704},{32,736},{64,0},{96,32},{128,64},{160,96},{192,128},{224,1... | collective-permute-start | bytes 1572872 | tf_op jit(solution)/shard_map/ppermute | solution.py:53
  30.4 10.6 %collective-permute-done.1 = bf16[4,32,2048]{2,1,0:T(8,128)(2,1)} collective-permute-done((bf16[4,32,2048]{2,1,0:T(8,128)(2,1)}, bf16[4,32,2048]{2,1,0:T(8,128)(2,1)}, u32[]{:S(2)}, u32[]{:S(2)}) %collective-permute-start.1) | collective-permute-done | bytes 524320 | tf_op jit(solution)/shard_map/ppermute | solution.py:52
  41.0 1.2 collective-permute-done.2
  42.1 2.5 %fusion.17 = bf16[4,32,2048]{2,1,0:T(8,128)(2,1)} fusion(bf16[4,32,2048]{2,1,0:T(8,128)(2,1)} %collective-permute-done.2, bf16[4,32,2048]{2,1,0:T(8,128)(2,1)} %collective-permute-done.1, bf16[4,3,32,2048]{3,2,0,1:T(8,128)(2,1)} %collective-permute-done, s32[]{:T(128)S(6)} %select_n.64, bf16[4,3,2,32,2048]{4,3,2,1,0:T(8,128)(2,1)S(1)} %bitcast.68, ...), kind=kLoop, calls=%fused_computation.31 | loop fusion | flops 2097152 | bytes 2621452 | tf_op jit(solution)/shard_map/convert_element_type | solution.py:54
  44.6 0.0 copy-start.1
  44.6 6.2 %all-to-all-start = ((bf16[4,32,2048]{2,1,0:T(8,128)(2,1)}), bf16[4,32,2048]{2,1,0:T(8,128)(2,1)S(1)}, u32[]{:S(2)}, u32[]{:S(2)}) async-start(bf16[4,32,2048]{2,1,0:T(8,128)(2,1)} %fusion.17), calls=%async_computation | async-start | bytes 1048576 | tf_op jit(solution)/shard_map/all_to_all | solution.py:55
  50.9 0.0 copy-done.2
  50.9 21.5 %all-to-all-done = bf16[4,32,2048]{2,1,0:T(8,128)(2,1)S(1)} async-done(((bf16[4,32,2048]{2,1,0:T(8,128)(2,1)}), bf16[4,32,2048]{2,1,0:T(8,128)(2,1)S(1)}, u32[]{:S(2)}, u32[]{:S(2)}) %all-to-all-start) | async-done | bytes 524320 | tf_op jit(solution)/shard_map/all_to_all | solution.py:55
  72.4 0.3 copy.27
  72.6 0.3 fusion.27
  72.9 0.9 copy.28
  73.8 10.2 %all-to-all-start.1 = ((f32[32,16,128]{2,1,0:T(8,128)}), f32[32,16,128]{2,1,0:T(8,128)S(1)}, u32[]{:S(2)}, u32[]{:S(2)}) async-start(f32[32,16,128]{2,1,0:T(8,128)} %copy.28), calls=%async_computation.1 | async-start | bytes 524288 | tf_op jit(solution)/shard_map/all_to_all | solution.py:104
  84.0 0.0 copy-done.1
  84.0 0.3 broadcast_multiply_fusion
  84.3 10.7 %all-to-all-done.1 = f32[32,16,128]{2,1,0:T(8,128)S(1)} async-done(((f32[32,16,128]{2,1,0:T(8,128)}), f32[32,16,128]{2,1,0:T(8,128)S(1)}, u32[]{:S(2)}, u32[]{:S(2)}) %all-to-all-start.1) | async-done | bytes 262176 | tf_op jit(solution)/shard_map/all_to_all | solution.py:104
  95.0 0.7 add_convert_fusion
  95.7 21.0 %all_gather.3 = bf16[128,2048]{1,0:T(8,128)(2,1)} all-gather(bf16[32,2048]{1,0:T(8,128)(2,1)S(1)} %bitcast.74), channel_id=1, replica_groups={{0,192,384,576},{32,224,416,608},{64,256,448,640},{96,288,480,672},{128..., dimensions={0}, use_global_device_ids=true | all-gather | bytes 655360 | tf_op jit(solution)/shard_map/all_gather | solution.py:60
  116.8 6.3 %collective-permute-start.3 = (bf16[128,2048]{1,0:T(8,128)(2,1)}, bf16[128,2048]{1,0:T(8,128)(2,1)}, u32[]{:S(2)}, u32[]{:S(2)}) collective-permute-start(bf16[128,2048]{1,0:T(8,128)(2,1)} %all_gather.3), channel_id=1, source_target_pairs={{0,64},{32,96},{64,128},{96,160},{128,192},{160,224},{192,256},{22... | collective-permute-start | bytes 1572872 | tf_op jit(solution)/shard_map/ppermute | solution.py:61
  123.0 1.9 %collective-permute-start.4 = (bf16[128,2048]{1,0:T(8,128)(2,1)}, bf16[128,2048]{1,0:T(8,128)(2,1)}, u32[]{:S(2)}, u32[]{:S(2)}) collective-permute-start(bf16[128,2048]{1,0:T(8,128)(2,1)} %all_gather.3), channel_id=1, source_target_pairs={{0,704},{32,736},{64,0},{96,32},{128,64},{160,96},{192,128},{224,1... | collective-permute-start | bytes 1572872 | tf_op jit(solution)/shard_map/ppermute | solution.py:62
  125.0 1.9 %collective-permute-start.5 = (bf16[128,2048]{1,0:T(8,128)(2,1)}, bf16[128,2048]{1,0:T(8,128)(2,1)S(1)}, u32[]{:S(2)}, u32[]{:S(2)}) collective-permute-start(bf16[128,2048]{1,0:T(8,128)(2,1)} %all_gather.3), channel_id=1, source_target_pairs={{0,32},{32,0},{64,96},{96,64},{128,160},{160,128},{192,224},{224,1... | collective-permute-start | bytes 1572872 | tf_op jit(solution)/shard_map/ppermute | solution.py:64
  126.9 1.1 constant_dynamic-update-slice_fusion.5
  128.0 2.0 %collective-permute-done.3 = bf16[128,2048]{1,0:T(8,128)(2,1)} collective-permute-done((bf16[128,2048]{1,0:T(8,128)(2,1)}, bf16[128,2048]{1,0:T(8,128)(2,1)}, u32[]{:S(2)}, u32[]{:S(2)}) %collective-permute-start.3) | collective-permute-done | bytes 524320 | tf_op jit(solution)/shard_map/ppermute | solution.py:61
  130.0 1.9 %collective-permute-start.6 = (bf16[128,2048]{1,0:T(8,128)(2,1)}, bf16[128,2048]{1,0:T(8,128)(2,1)S(1)}, u32[]{:S(2)}, u32[]{:S(2)}) collective-permute-start(bf16[128,2048]{1,0:T(8,128)(2,1)} %collective-permute-done.3), channel_id=1, source_target_pairs={{0,32},{32,0},{64,96},{96,64},{128,160},{160,128},{192,224},{224,1... | collective-permute-start | bytes 1572872 | tf_op jit(solution)/shard_map/ppermute | solution.py:64
  132.0 1.1 constant_dynamic-update-slice_fusion.4
  133.0 1.4 collective-permute-done.4
  134.4 1.9 %collective-permute-start.7 = (bf16[128,2048]{1,0:T(8,128)(2,1)}, bf16[128,2048]{1,0:T(8,128)(2,1)S(1)}, u32[]{:S(2)}, u32[]{:S(2)}) collective-permute-start(bf16[128,2048]{1,0:T(8,128)(2,1)} %collective-permute-done.4), channel_id=1, source_target_pairs={{0,32},{32,0},{64,96},{96,64},{128,160},{160,128},{192,224},{224,1... | collective-permute-start | bytes 1572872 | tf_op jit(solution)/shard_map/ppermute | solution.py:64
  136.4 1.1 constant_dynamic-update-slice_fusion.3
  137.4 0.0 collective-permute-done.5
  137.5 0.0 collective-permute-done.6
  137.6 0.9 collective-permute-done.7
  138.5 4.7 %select_reduce_fusion = (f32[]{:T(128)}, f32[768,768]{1,0:T(8,128)}) fusion(bf16[768,2048]{1,0:T(8,128)(2,1)S(1)} %constant_dynamic-update-slice_fusion), kind=kOutput, calls=%fused_computation.8 | convolution fusion | flops 2417688576 | bytes 5505028 | tf_op jit(solution)/shard_map/dot_general | solution.py:69
  143.9 1.9 %multiply_convert_fusion = bf16[768,768]{1,0:T(8,128)(2,1)S(1)} fusion(f32[768,768]{1,0:T(8,128)} %get-tuple-element.13, f32[]{:T(128)S(6)} %div.17), kind=kLoop, calls=%fused_computation.7 | loop fusion | flops 1769472 | bytes 3538948 | tf_op jit(solution)/shard_map/convert_element_type | solution.py:73
  145.8 1.1 fusion.1
  146.9 0.0 copy-start
  146.9 1.1 convolution_convert_fusion.1
  148.0 0.0 copy-done
  148.0 1.2 fusion.4
  149.2 0.3 fusion.11
  149.5 2.2 %fusion.9 = bf16[4,8,16,128]{3,1,2,0:T(8,128)(2,1)S(1)} fusion(bf16[768,2048]{1,0:T(8,128)(2,1)S(1)} %constant_dynamic-update-slice_fusion, bf16[32,768]{1,0:T(8,128)(2,1)S(1)} %fusion.11, bf16[768,768]{1,0:T(8,128)(2,1)} %copy-done, f32[]{:T(128)S(6)} %div.17, s32[]{:T(128)S(6)} %select_n.78, bf16[4,8,16,128]{3,2,1,0:T(8,128)(2,1)S(1)} %bitcast.72), kind=kOutput, calls=%fused_computation.18 | convolution fusion | flops 138952704 | bytes 4734984 | tf_op jit(solution)/shard_map/dot_general | solution.py:76
  151.7 15.4 %all_to_all.15 = bf16[32,16,128]{2,1,0:T(8,128)(2,1)S(1)} all-to-all(bf16[32,16,128]{2,1,0:T(8,128)(2,1)S(1)} %bitcast.75), channel_id=1, replica_groups=mesh['rep'=24,'fsdp'=32] {'fsdp'}, dimensions={0} | all-to-all | bytes 262144 | tf_op jit(solution)/shard_map/all_to_all | solution.py:112
  167.1 0.9 fusion.8
  (6 shorter events, 0.2 us)
Async XLA Ops:
  5.5 5.6 %collective-permute-start = (bf16[4,3,32,2048]{3,2,0,1:T(8,128)(2,1)}, bf16[4,3,32,2048]{3,2,0,1:T(8,128)(2,1)}, u32[]{:S(2)}, u32[]{:S(2)}) collective-permute-start(bf16[4,3,32,2048]{3,2,0,1:T(8,128)(2,1)} %copy_bitcast_fusion), channel_id=1, source_target_pairs={{0,32},{32,0},{64,96},{96,64},{128,160},{160,128},{192,224},{224,1... | collective-permute-start | bytes 4718600 | tf_op jit(solution)/shard_map/ppermute | solution.py:47
  13.7 37.1 %copy-start.2 = (s32[32]{0:T(128)S(1)}, s32[32]{0:T(128)}, u32[]{:S(2)}) copy-start(s32[32]{0:T(128)} %param.5) | copy-start | bytes 388
  13.7 27.2 %collective-permute-start.1 = (bf16[4,32,2048]{2,1,0:T(8,128)(2,1)}, bf16[4,32,2048]{2,1,0:T(8,128)(2,1)}, u32[]{:S(2)}, u32[]{:S(2)}) collective-permute-start(bf16[4,32,2048]{2,1,0:T(8,128)(2,1)} %get-tuple-element.10), channel_id=1, source_target_pairs={{0,64},{32,96},{64,128},{96,160},{128,192},{160,224},{192,256},{22... | collective-permute-start | bytes 1572872 | tf_op jit(solution)/shard_map/ppermute | solution.py:52
  18.1 24.0 %collective-permute-start.2 = (bf16[4,32,2048]{2,1,0:T(8,128)(2,1)}, bf16[4,32,2048]{2,1,0:T(8,128)(2,1)}, u32[]{:S(2)}, u32[]{:S(2)}) collective-permute-start(bf16[4,32,2048]{2,1,0:T(8,128)(2,1)} %get-tuple-element.11), channel_id=1, source_target_pairs={{0,704},{32,736},{64,0},{96,32},{128,64},{160,96},{192,128},{224,1... | collective-permute-start | bytes 1572872 | tf_op jit(solution)/shard_map/ppermute | solution.py:53
  44.6 39.4 %copy-start.1 = (f32[1,32,1,2048]{3,2,1,0:T(1,128)S(1)}, f32[1,32,1,2048]{3,2,1,0:T(1,128)}, u32[]{:S(2)}) copy-start(f32[1,32,1,2048]{3,2,1,0:T(1,128)} %param.4) | copy-start | bytes 786436
  44.6 27.7 %all-to-all-start = ((bf16[4,32,2048]{2,1,0:T(8,128)(2,1)}), bf16[4,32,2048]{2,1,0:T(8,128)(2,1)S(1)}, u32[]{:S(2)}, u32[]{:S(2)}) async-start(bf16[4,32,2048]{2,1,0:T(8,128)(2,1)} %fusion.17), calls=%async_computation | async-start | bytes 1048576 | tf_op jit(solution)/shard_map/all_to_all | solution.py:55
  73.8 21.2 %all-to-all-start.1 = ((f32[32,16,128]{2,1,0:T(8,128)}), f32[32,16,128]{2,1,0:T(8,128)S(1)}, u32[]{:S(2)}, u32[]{:S(2)}) async-start(f32[32,16,128]{2,1,0:T(8,128)} %copy.28), calls=%async_computation.1 | async-start | bytes 524288 | tf_op jit(solution)/shard_map/all_to_all | solution.py:104
  116.8 13.3 %collective-permute-start.3 = (bf16[128,2048]{1,0:T(8,128)(2,1)}, bf16[128,2048]{1,0:T(8,128)(2,1)}, u32[]{:S(2)}, u32[]{:S(2)}) collective-permute-start(bf16[128,2048]{1,0:T(8,128)(2,1)} %all_gather.3), channel_id=1, source_target_pairs={{0,64},{32,96},{64,128},{96,160},{128,192},{160,224},{192,256},{22... | collective-permute-start | bytes 1572872 | tf_op jit(solution)/shard_map/ppermute | solution.py:61
  123.0 11.4 %collective-permute-start.4 = (bf16[128,2048]{1,0:T(8,128)(2,1)}, bf16[128,2048]{1,0:T(8,128)(2,1)}, u32[]{:S(2)}, u32[]{:S(2)}) collective-permute-start(bf16[128,2048]{1,0:T(8,128)(2,1)} %all_gather.3), channel_id=1, source_target_pairs={{0,704},{32,736},{64,0},{96,32},{128,64},{160,96},{192,128},{224,1... | collective-permute-start | bytes 1572872 | tf_op jit(solution)/shard_map/ppermute | solution.py:62
  125.0 12.4 %collective-permute-start.5 = (bf16[128,2048]{1,0:T(8,128)(2,1)}, bf16[128,2048]{1,0:T(8,128)(2,1)S(1)}, u32[]{:S(2)}, u32[]{:S(2)}) collective-permute-start(bf16[128,2048]{1,0:T(8,128)(2,1)} %all_gather.3), channel_id=1, source_target_pairs={{0,32},{32,0},{64,96},{96,64},{128,160},{160,128},{192,224},{224,1... | collective-permute-start | bytes 1572872 | tf_op jit(solution)/shard_map/ppermute | solution.py:64
  130.0 7.5 %collective-permute-start.6 = (bf16[128,2048]{1,0:T(8,128)(2,1)}, bf16[128,2048]{1,0:T(8,128)(2,1)S(1)}, u32[]{:S(2)}, u32[]{:S(2)}) collective-permute-start(bf16[128,2048]{1,0:T(8,128)(2,1)} %collective-permute-done.3), channel_id=1, source_target_pairs={{0,32},{32,0},{64,96},{96,64},{128,160},{160,128},{192,224},{224,1... | collective-permute-start | bytes 1572872 | tf_op jit(solution)/shard_map/ppermute | solution.py:64
  134.4 4.0 %collective-permute-start.7 = (bf16[128,2048]{1,0:T(8,128)(2,1)}, bf16[128,2048]{1,0:T(8,128)(2,1)S(1)}, u32[]{:S(2)}, u32[]{:S(2)}) collective-permute-start(bf16[128,2048]{1,0:T(8,128)(2,1)} %collective-permute-done.4), channel_id=1, source_target_pairs={{0,32},{32,0},{64,96},{96,64},{128,160},{160,128},{192,224},{224,1... | collective-permute-start | bytes 1572872 | tf_op jit(solution)/shard_map/ppermute | solution.py:64
  146.9 1.1 copy-start

commit v2 on v1

v2 whole, which is shorter than its diff:
```python
import math

import jax
import jax.numpy as jnp
from jax import lax
from jax.experimental import pallas as pl
from jax.experimental.pallas import tpu as pltpu
from jax.sharding import PartitionSpec as P

DECAY_RATE = 0.95
NEWTON_A = 3.4445
NEWTON_B = -4.775
NEWTON_C = 2.0315
EPSILON = 1e-07

STRIDE = 3

F32 = jnp.float32
BF16 = jnp.bfloat16

SCALARS = pl.BlockSpec(memory_space=pltpu.SMEM)
VECTORS = pl.BlockSpec(memory_space=pltpu.VMEM)


def grant(mebibytes):
    return pltpu.CompilerParams(vmem_limit_bytes=mebibytes * 2**20)


def shift(chips, replicas):
    return [(r, (r + 2 * chips) % replicas) for r in range(replicas)]


def other_core(replicas):
    return [(r, r ^ 1) for r in range(replicas)]


def classes(replicas):
    chips = replicas // 2
    return [
        [2 * z + core for z in range(first, chips, STRIDE)]
        for first in range(STRIDE)
        for core in range(2)
    ]


def pick(array, index, axis):
    return lax.dynamic_index_in_dim(array, index, axis, keepdims=False)


def chip_sums_kernel(replica_ref, mine_ref, theirs_ref, up_ref, down_ref):
    core = lax.rem(replica_ref[0], 2)
    kind = lax.rem(lax.div(replica_ref[0], 2), STRIDE)
    for step, out_ref in ((1, up_ref), (2, down_ref)):
        there = lax.rem(kind + step, STRIDE)
        for n in range(out_ref.shape[0]):
            out_ref[n] = (mine_ref[n, there, core].astype(F32) + theirs_ref[n, there].astype(F32)).astype(BF16)


def cluster_sums_kernel(replica_ref, mine_ref, theirs_ref, below_ref, above_ref, *out_refs):
    core = lax.rem(replica_ref[0], 2)
    chip = lax.div(replica_ref[0], 2)
    kind, place = lax.rem(chip, STRIDE), lax.div(chip, STRIDE)
    for step, out_ref in enumerate(out_refs):
        n = lax.rem(place + step, len(out_refs))
        total = mine_ref[n, kind, core].astype(F32) + theirs_ref[n, kind].astype(F32)
        out_ref[...] = (total + below_ref[n].astype(F32) + above_ref[n].astype(F32)).astype(BF16)


def place_kernel(owner_ref, *refs):
    parts, out_ref = refs[:-1], refs[-1]
    slots, tiles, lanes = out_ref.shape
    slot = lax.broadcasted_iota(jnp.int32, (slots, slots), 0)
    onehot = jnp.where(slot == owner_ref[...], 1.0, 0.0).astype(BF16)
    total = product(onehot, parts[0][...])
    for part in parts[1:]:
        total += product(onehot, part[...])
    for tile in range(tiles):
        out_ref[:, tile, :] = total[:, tile * lanes : (tile + 1) * lanes]


def sum_rows(grads, owner, replica, replicas, lanes):
    experts, _, width = grads.shape
    members = replicas // (2 * STRIDE)
    here = replica.reshape(1)
    mine = grads.transpose(1, 0, 2).reshape(members, STRIDE, 2, experts, width)
    theirs = lax.ppermute(pick(mine, 1 - replica % 2, 2), "rep", other_core(replicas))
    some = jax.ShapeDtypeStruct((members, experts, width), BF16)
    up, down = pl.pallas_call(
        chip_sums_kernel,
        out_shape=(some, some),
        in_specs=[SCALARS, VECTORS, VECTORS],
        out_specs=(VECTORS, VECTORS),
        compiler_params=grant(12),
        name="chip_sums",
    )(here, mine, theirs)
    below = lax.ppermute(up, "rep", shift(1, replicas))
    above = lax.ppermute(down, "rep", shift(-1, replicas))
    sums = pl.pallas_call(
        cluster_sums_kernel,
        out_shape=(jax.ShapeDtypeStruct((experts, width), BF16),) * members,
        in_specs=[SCALARS] + [VECTORS] * 4,
        out_specs=(VECTORS,) * members,
        compiler_params=grant(12),
        name="cluster_sums",
    )(here, mine, theirs, below, above)
    parts = [sums[0]]
    for step in sorted(range(1, members), key=lambda n: abs(2 * n - members), reverse=True):
        parts.append(lax.ppermute(sums[step], "rep", shift(STRIDE * step, replicas)))
    return pl.pallas_call(
        place_kernel,
        out_shape=jax.ShapeDtypeStruct((experts, width // lanes, lanes), F32),
        in_specs=[VECTORS] * (1 + members),
        out_specs=VECTORS,
        compiler_params=grant(4),
        name="place",
    )(owner.reshape(1, -1), *parts)


def gather_rows(rows, replicas):
    own = lax.all_gather(rows, "rep", axis=0, tiled=True, axis_index_groups=classes(replicas))
    below = lax.ppermute(own, "rep", shift(1, replicas))
    above = lax.ppermute(own, "rep", shift(-1, replicas))
    pieces = [own, below, above]
    return pieces + [lax.ppermute(piece, "rep", other_core(replicas)) for piece in pieces]


def product(a, b):
    return lax.dot_general(a, b, (((1,), (0,)), ((), ())), preferred_element_type=F32)


def newton_kernel(count, factor, first_ref, *refs):
    pieces, (out_ref, x_ref, raw_ref, gram_ref, poly_ref, mixed_ref, next_ref) = refs[:-7], refs[-7:]
    height = pieces[0].shape[0]
    for n, piece in enumerate(pieces):
        x_ref[pl.ds(n * height, height), :] = piece[...]
    size = x_ref.shape[0]
    step = 2 * height
    blocks = [pl.ds(n * step, step) for n in range(size // step)]
    diagonal = lax.broadcasted_iota(jnp.int32, (step, step), 0) == lax.broadcasted_iota(jnp.int32, (step, step), 1)
    trace = jnp.float32(0.0)
    for n, block in enumerate(blocks):
        raw = lax.dot_general(x_ref[block, :], x_ref[...], (((1,), (1,)), ((), ())), preferred_element_type=F32)
        raw_ref[block, :] = raw
        trace += jnp.sum(jnp.where(diagonal, raw[:, n * step : (n + 1) * step], 0.0))
    scale = 1.0 / (jnp.sqrt(trace) + EPSILON)
    for block in blocks:
        gram_ref[block, :] = (raw_ref[block, :] * scale * scale).astype(BF16)
    for block in blocks:
        squared = product(gram_ref[block, :], gram_ref[...])
        poly_ref[block, :] = (NEWTON_B * gram_ref[block, :].astype(F32) + NEWTON_C * squared).astype(BF16)
    for block in blocks:
        mixed_ref[block, :] = product(gram_ref[block, :], poly_ref[...]).astype(BF16)
    for block in blocks:
        own = NEWTON_A * NEWTON_A * gram_ref[block, :].astype(F32) + 2.0 * NEWTON_A * mixed_ref[block, :].astype(F32)
        next_ref[block, :] = (own + product(mixed_ref[block, :], poly_ref[...])).astype(BF16)
    rows = pl.ds(pl.multiple_of(first_ref[0], count), count)
    own_gram = next_ref[rows, :]
    own_poly = NEWTON_B * own_gram.astype(F32) + NEWTON_C * product(own_gram, next_ref[...])
    own_poly = own_poly.astype(BF16)
    weights = NEWTON_A * (poly_ref[rows, :].astype(F32) + own_poly.astype(F32)) + product(own_poly, poly_ref[...])
    result = NEWTON_A * NEWTON_A * x_ref[rows, :].astype(F32) + product(weights.astype(BF16), x_ref[...])
    out_ref[...] = (factor * scale * result).astype(BF16)


def newton_rows(pieces, count, first_row, factor):
    height, width = pieces[0].shape
    size = height * len(pieces)
    square = pltpu.VMEM((size, size), BF16)
    return pl.pallas_call(
        lambda *refs: newton_kernel(count, factor, *refs),
        out_shape=jax.ShapeDtypeStruct((count, width), BF16),
        in_specs=[SCALARS] + [VECTORS] * len(pieces),
        out_specs=VECTORS,
        scratch_shapes=[pltpu.VMEM((size, width), BF16), pltpu.VMEM((size, size), F32), square, square, square, square],
        compiler_params=grant(20),
        name="newton",
    )(first_row.reshape(1), *pieces)


def on_device(grads, momentum, owner):
    slots = lax.axis_size("fsdp")
    replicas = lax.axis_size("rep")
    replica = lax.axis_index("rep")
    width = grads.shape[-1]
    lanes = math.gcd(width, 128)
    tiled = (slots, width // lanes, lanes)

    outgoing = sum_rows(grads[0], owner, replica, replicas, lanes)
    grad_rows = lax.all_to_all(outgoing, "fsdp", split_axis=0, concat_axis=0, tiled=True)
    moment_new = DECAY_RATE * momentum.reshape(tiled) + grad_rows
    nesterov = (grad_rows + DECAY_RATE * moment_new).astype(BF16).reshape(slots, width)

    pieces = gather_rows(nesterov, replicas)
    update_rows = newton_rows(pieces, slots, (replica // (2 * STRIDE)) * slots, math.sqrt(width))

    returning = lax.all_to_all(update_rows.reshape(tiled), "fsdp", split_axis=0, concat_axis=0, tiled=True)
    onehot = (owner[None, :] == jnp.arange(slots, dtype=jnp.int32)[:, None]).astype(BF16)
    updates = jnp.einsum(
        "se,sd->ed", onehot, returning.reshape(slots, width), preferred_element_type=F32
    ).astype(BF16)
    return (updates[:, None, None], moment_new.reshape(momentum.shape))


def solution(mesh):
    placed = (P("rep", None, "fsdp", None), P("fsdp", None, "rep", None), P())
    return jax.shard_map(
        on_device,
        mesh=mesh,
        in_specs=placed,
        out_specs=(P(None, "fsdp", "rep", None), P("fsdp", None, "rep", None)),
        check_vma=False,
    )
```

time: 169 us -> 154 us (0.911)
  matrix products: 11.7 us -> 0.89 us
  waiting for transfers between devices: 51.9 us -> 42.1 us
  starting transfers between devices: 48.9 us -> 58 us
  Pallas kernels: 0 us -> 9.08 us
  other arithmetic: 7.96 us -> 1.02 us
  local copies, waits for them, and re-layouts: 9.41 us -> 3.79 us
    all_to_all x2 -> x1, waiting for transfers between devices: 32.2 us -> 10.8 us  [on_device(): lax.all_to_all(outgoing, 'fsdp', split_axis=0, concat_axis=0, tiled=True)]
    ppermute x8 -> x11, starting transfers between devices: 32.5 us -> 47.8 us  [the longest x3 15.6 us: sum_rows(): lax.ppermute(sums[step], 'rep', shift(STRIDE * step, replicas))]
    ppermute x8 -> x11, waiting for transfers between devices: 19.7 us -> 31.3 us  [the longest x1 10.1 us: sum_rows(): below = lax.ppermute(up, 'rep', shift(1, replicas))]
    dot_general x7 -> x0, matrix products: 10.9 us -> none  [the longest x5 5.89 us: dot(): return jnp.dot(a, b, preferred_element_type=F32)]
    pallas_call x0 -> x4, Pallas kernels: none -> 9.08 us  [the longest x1 7.5 us: newton_rows(): pl.pallas_call(lambda *refs: newton_kernel(count, factor, *refs), out_sha...]
    convert_element_type x3 -> x0, other arithmetic: 6.94 us -> none  [the longest x1 2.55 us: sum_rows(): chip_sum((kind + 1) % STRIDE).astype(BF16)]
    unnamed x14 -> x6, local copies, waits for them, and re-layouts: 6.99 us -> 0.07 us
    all_to_all x2 -> x1, starting transfers between devices: 16.4 us -> 10.2 us  [on_device(): lax.all_to_all(outgoing, 'fsdp', split_axis=0, concat_axis=0, tiled=True)]
  transfers between devices with their start and end apart: 10 -> 12, of which waited for: 8 -> 9; matrix products, arithmetic and copies ran while one was open for 2% -> 0% of each run, Pallas kernels for 0% -> 0%
where the time goes in v2:
time: 154 us
  starting transfers between devices  58 us (38%)
  waiting for transfers between devices  42.1 us (27%)
  blocking collectives  38 us (25%)
  Pallas kernels  9.08 us (6%)
  local copies, waits for them, and re-layouts  3.79 us (2%)
    all_gather x1, blocking collectives, gather_rows(): lax.all_gather(rows, 'rep', axis=0, tiled=True, axis_index_groups=classes...  23.3 us
    ppermute x3, starting transfers between devices, sum_rows(): lax.ppermute(sums[step], 'rep', shift(STRIDE * step, replicas))  15.6 us
    all_to_all x1, blocking collectives, on_device(): lax.all_to_all(update_rows.reshape(tiled), 'fsdp', split_axis=0, concat_a...  14.7 us
    ppermute x1, starting transfers between devices, sum_rows(): above = lax.ppermute(down, 'rep', shift(-1, replicas))  12.4 us
    all_to_all x1, waiting for transfers between devices, on_device(): lax.all_to_all(outgoing, 'fsdp', split_axis=0, concat_axis=0, tiled=True)  10.8 us
    all_to_all x1, starting transfers between devices, on_device(): lax.all_to_all(outgoing, 'fsdp', split_axis=0, concat_axis=0, tiled=True)  10.2 us
    ppermute x1, waiting for transfers between devices, sum_rows(): below = lax.ppermute(up, 'rep', shift(1, replicas))  10.1 us
    ppermute x3, waiting for transfers between devices, sum_rows(): lax.ppermute(sums[step], 'rep', shift(STRIDE * step, replicas))  8.14 us
  transfers between devices with their start and end apart: 12, of which 9 were waited for; matrix products, arithmetic and copies ran while one was open for 0% of the time, Pallas kernels for 0%

profile of v2, /device:TPU:8, one launch (start us, length us, event | category | flops | bytes accessed | tf_op | source)
XLA Modules:
  0.0 153.7 jit_solution(998287732575515695)
XLA Ops:
  0.6 3.6 %copy.5 = bf16[24,32,2048]{2,1,0:T(8,128)(2,1)S(1)} copy(bf16[24,32,2048]{2,0,1:T(8,128)(2,1)} %bitcast.28) | data formatting | bytes 6291456 | tf_op jit(solution)/shard_map/transpose | solution.py:85
  4.3 0.1 dynamic-slice_bitcast_fusion
  4.4 1.9 %collective-permute-start = (bf16[4,3,32,2048]{3,2,1,0:T(8,128)(2,1)S(1)}, bf16[4,3,32,2048]{3,2,1,0:T(8,128)(2,1)S(1)}, u32[]{:S(2)}, u32[]{:S(2)}) collective-permute-start(bf16[4,3,32,2048]{3,2,1,0:T(8,128)(2,1)S(1)} %dynamic-slice_bitcast_fusion), channel_id=1, source_target_pairs={{0,32},{32,0},{64,96},{96,64},{128,160},{160,128},{192,224},{224,1... | collective-permute-start | bytes 4718600 | tf_op jit(solution)/shard_map/ppermute | solution.py:86
  6.3 3.4 %collective-permute-done.theirs_ref = bf16[4,3,32,2048]{3,2,1,0:T(8,128)(2,1)S(1)} collective-permute-done((bf16[4,3,32,2048]{3,2,1,0:T(8,128)(2,1)S(1)}, bf16[4,3,32,2048]{3,2,1,0:T(8,128)(2,1)S(1)}, u32[]{:S(2)}, u32[]{:S(2)}) %collective-permute-start) | collective-permute-done | bytes 1572896 | tf_op jit(solution)/shard_map/ppermute | solution.py:86
  9.7 0.2 chip_sums.1
  9.9 0.0 copy-start
  9.9 4.3 %collective-permute-start.1 = (bf16[4,32,2048]{2,1,0:T(8,128)(2,1)S(1)}, bf16[4,32,2048]{2,1,0:T(8,128)(2,1)S(1)}, u32[]{:S(2)}, u32[]{:S(2)}) collective-permute-start(bf16[4,32,2048]{2,1,0:T(8,128)(2,1)S(1)} %get-tuple-element.8), channel_id=1, source_target_pairs={{0,64},{32,96},{64,128},{96,160},{128,192},{160,224},{192,256},{22... | collective-permute-start | bytes 1572872 | tf_op jit(solution)/shard_map/ppermute | solution.py:96
  14.2 0.0 copy-start.1
  14.2 12.4 %collective-permute-start.2 = (bf16[4,32,2048]{2,1,0:T(8,128)(2,1)S(1)}, bf16[4,32,2048]{2,1,0:T(8,128)(2,1)S(1)}, u32[]{:S(2)}, u32[]{:S(2)}) collective-permute-start(bf16[4,32,2048]{2,1,0:T(8,128)(2,1)S(1)} %get-tuple-element.9), channel_id=1, source_target_pairs={{0,704},{32,736},{64,0},{96,32},{128,64},{160,96},{192,128},{224,1... | collective-permute-start | bytes 1572872 | tf_op jit(solution)/shard_map/ppermute | solution.py:97
  26.6 10.1 %collective-permute-done.1.below_ref = bf16[4,32,2048]{2,1,0:T(8,128)(2,1)S(1)} collective-permute-done((bf16[4,32,2048]{2,1,0:T(8,128)(2,1)S(1)}, bf16[4,32,2048]{2,1,0:T(8,128)(2,1)S(1)}, u32[]{:S(2)}, u32[]{:S(2)}) %collective-permute-start.1) | collective-permute-done | bytes 524320 | tf_op jit(solution)/shard_map/ppermute | solution.py:96
  36.8 1.3 collective-permute-done.2.above_ref
  38.1 0.3 cluster_sums.1
  38.3 2.2 %collective-permute-start.3 = (bf16[32,2048]{1,0:T(8,128)(2,1)S(1)}, bf16[32,2048]{1,0:T(8,128)(2,1)S(1)}, u32[]{:S(2)}, u32[]{:S(2)}) collective-permute-start(bf16[32,2048]{1,0:T(8,128)(2,1)S(1)} %get-tuple-element.11), channel_id=1, source_target_pairs={{0,192},{32,224},{64,256},{96,288},{128,320},{160,352},{192,384},{... | collective-permute-start | bytes 393224 | tf_op jit(solution)/shard_map/ppermute | solution.py:108
  40.5 6.6 %collective-permute-start.4 = (bf16[32,2048]{1,0:T(8,128)(2,1)S(1)}, bf16[32,2048]{1,0:T(8,128)(2,1)S(1)}, u32[]{:S(2)}, u32[]{:S(2)}) collective-permute-start(bf16[32,2048]{1,0:T(8,128)(2,1)S(1)} %get-tuple-element.12), channel_id=1, source_target_pairs={{0,576},{32,608},{64,640},{96,672},{128,704},{160,736},{192,0},{22... | collective-permute-start | bytes 393224 | tf_op jit(solution)/shard_map/ppermute | solution.py:108
  47.2 6.7 %collective-permute-start.5 = (bf16[32,2048]{1,0:T(8,128)(2,1)S(1)}, bf16[32,2048]{1,0:T(8,128)(2,1)S(1)}, u32[]{:S(2)}, u32[]{:S(2)}) collective-permute-start(bf16[32,2048]{1,0:T(8,128)(2,1)S(1)} %get-tuple-element.13), channel_id=1, source_target_pairs={{0,384},{32,416},{64,448},{96,480},{128,512},{160,544},{192,576},{... | collective-permute-start | bytes 393224 | tf_op jit(solution)/shard_map/ppermute | solution.py:108
  53.9 0.0 collective-permute-done.3.refs_1_
  54.0 7.4 %collective-permute-done.4.refs_2_ = bf16[32,2048]{1,0:T(8,128)(2,1)S(1)} collective-permute-done((bf16[32,2048]{1,0:T(8,128)(2,1)S(1)}, bf16[32,2048]{1,0:T(8,128)(2,1)S(1)}, u32[]{:S(2)}, u32[]{:S(2)}) %collective-permute-start.4) | collective-permute-done | bytes 131104 | tf_op jit(solution)/shard_map/ppermute | solution.py:108
  61.4 0.7 collective-permute-done.5.refs_3_
  62.1 0.0 copy-done
  62.1 1.1 place.1
  63.2 10.2 %all-to-all-start = ((f32[32,16,128]{2,1,0:T(8,128)}), f32[32,16,128]{2,1,0:T(8,128)S(1)}, u32[]{:S(2)}, u32[]{:S(2)}) async-start(f32[32,16,128]{2,1,0:T(8,128)} %place.1), calls=%async_computation | async-start | bytes 524288 | tf_op jit(solution)/shard_map/all_to_all | solution.py:189
  73.4 0.0 copy-done.1
  73.4 0.3 broadcast_multiply_fusion
  73.6 10.8 %all-to-all-done = f32[32,16,128]{2,1,0:T(8,128)S(1)} async-done(((f32[32,16,128]{2,1,0:T(8,128)}), f32[32,16,128]{2,1,0:T(8,128)S(1)}, u32[]{:S(2)}, u32[]{:S(2)}) %all-to-all-start) | async-done | bytes 262176 | tf_op jit(solution)/shard_map/all_to_all | solution.py:189
  84.4 0.7 add_convert_fusion
  85.2 23.3 %all_gather.3.refs_1_ = bf16[128,2048]{1,0:T(8,128)(2,1)S(1)} all-gather(bf16[32,2048]{1,0:T(8,128)(2,1)S(1)} %bitcast.31), channel_id=1, replica_groups={{0,192,384,576},{32,224,416,608},{64,256,448,640},{96,288,480,672},{128..., dimensions={0}, use_global_device_ids=true | all-gather | bytes 655360 | tf_op jit(solution)/shard_map/all_gather | solution.py:120
  108.5 6.0 %collective-permute-start.7 = (bf16[128,2048]{1,0:T(8,128)(2,1)S(1)}, bf16[128,2048]{1,0:T(8,128)(2,1)S(1)}, u32[]{:S(2)}, u32[]{:S(2)}) collective-permute-start(bf16[128,2048]{1,0:T(8,128)(2,1)S(1)} %all_gather.3.refs_1_), channel_id=1, source_target_pairs={{0,704},{32,736},{64,0},{96,32},{128,64},{160,96},{192,128},{224,1... | collective-permute-start | bytes 1572872 | tf_op jit(solution)/shard_map/ppermute | solution.py:122
  114.5 1.9 %collective-permute-start.6 = (bf16[128,2048]{1,0:T(8,128)(2,1)S(1)}, bf16[128,2048]{1,0:T(8,128)(2,1)S(1)}, u32[]{:S(2)}, u32[]{:S(2)}) collective-permute-start(bf16[128,2048]{1,0:T(8,128)(2,1)S(1)} %all_gather.3.refs_1_), channel_id=1, source_target_pairs={{0,64},{32,96},{64,128},{96,160},{128,192},{160,224},{192,256},{22... | collective-permute-start | bytes 1572872 | tf_op jit(solution)/shard_map/ppermute | solution.py:121
  116.5 1.9 %collective-permute-start.8 = (bf16[128,2048]{1,0:T(8,128)(2,1)S(1)}, bf16[128,2048]{1,0:T(8,128)(2,1)S(1)}, u32[]{:S(2)}, u32[]{:S(2)}) collective-permute-start(bf16[128,2048]{1,0:T(8,128)(2,1)S(1)} %all_gather.3.refs_1_), channel_id=1, source_target_pairs={{0,32},{32,0},{64,96},{96,64},{128,160},{160,128},{192,224},{224,1... | collective-permute-start | bytes 1572872 | tf_op jit(solution)/shard_map/ppermute | solution.py:124
  118.4 2.8 %collective-permute-done.7.refs_3_ = bf16[128,2048]{1,0:T(8,128)(2,1)S(1)} collective-permute-done((bf16[128,2048]{1,0:T(8,128)(2,1)S(1)}, bf16[128,2048]{1,0:T(8,128)(2,1)S(1)}, u32[]{:S(2)}, u32[]{:S(2)}) %collective-permute-start.7) | collective-permute-done | bytes 524320 | tf_op jit(solution)/shard_map/ppermute | solution.py:122
  121.2 1.9 %collective-permute-start.10 = (bf16[128,2048]{1,0:T(8,128)(2,1)S(1)}, bf16[128,2048]{1,0:T(8,128)(2,1)S(1)}, u32[]{:S(2)}, u32[]{:S(2)}) collective-permute-start(bf16[128,2048]{1,0:T(8,128)(2,1)S(1)} %collective-permute-done.7.refs_3_), channel_id=1, source_target_pairs={{0,32},{32,0},{64,96},{96,64},{128,160},{160,128},{192,224},{224,1... | collective-permute-start | bytes 1572872 | tf_op jit(solution)/shard_map/ppermute | solution.py:124
  123.1 3.7 %collective-permute-done.6.refs_2_ = bf16[128,2048]{1,0:T(8,128)(2,1)S(1)} collective-permute-done((bf16[128,2048]{1,0:T(8,128)(2,1)S(1)}, bf16[128,2048]{1,0:T(8,128)(2,1)S(1)}, u32[]{:S(2)}, u32[]{:S(2)}) %collective-permute-start.6) | collective-permute-done | bytes 524320 | tf_op jit(solution)/shard_map/ppermute | solution.py:121
  126.8 1.9 %collective-permute-start.9 = (bf16[128,2048]{1,0:T(8,128)(2,1)S(1)}, bf16[128,2048]{1,0:T(8,128)(2,1)S(1)}, u32[]{:S(2)}, u32[]{:S(2)}) collective-permute-start(bf16[128,2048]{1,0:T(8,128)(2,1)S(1)} %collective-permute-done.6.refs_2_), channel_id=1, source_target_pairs={{0,32},{32,0},{64,96},{96,64},{128,160},{160,128},{192,224},{224,1... | collective-permute-start | bytes 1572872 | tf_op jit(solution)/shard_map/ppermute | solution.py:124
  128.8 0.0 collective-permute-done.8.refs_4_
  128.8 0.0 collective-permute-done.10.refs_6_
  128.8 1.8 %collective-permute-done.9.refs_5_ = bf16[128,2048]{1,0:T(8,128)(2,1)S(1)} collective-permute-done((bf16[128,2048]{1,0:T(8,128)(2,1)S(1)}, bf16[128,2048]{1,0:T(8,128)(2,1)S(1)}, u32[]{:S(2)}, u32[]{:S(2)}) %collective-permute-start.9) | collective-permute-done | bytes 524320 | tf_op jit(solution)/shard_map/ppermute | solution.py:124
  130.6 7.5 %newton.1 = bf16[32,2048]{1,0:T(8,128)(2,1)S(1)} custom-call(s32[1]{0:T(128)} %bitcast.refs_0_, bf16[128,2048]{1,0:T(8,128)(2,1)S(1)} %all_gather.3.refs_1_, bf16[128,2048]{1,0:T(8,128)(2,1)S(1)} %collective-permute-done.6.refs_2_, bf16[128,2048]{1,0:T(8,128)(2,1)S(1)} %collective-permute-done.7.refs_3_, ...), custom_call_target="tpu_custom_call" | custom-call | tf_op jit(solution)/shard_map/newton/pallas_call | solution.py:169
  138.1 14.7 %all_to_all.10 = bf16[32,16,128]{2,1,0:T(8,128)(2,1)S(1)} all-to-all(bf16[32,16,128]{2,1,0:T(8,128)(2,1)S(1)} %bitcast.32), channel_id=1, replica_groups=mesh['rep'=24,'fsdp'=32] {'fsdp'}, dimensions={0} | all-to-all | bytes 262144 | tf_op jit(solution)/shard_map/all_to_all | solution.py:196
  152.8 0.9 fusion
  (2 shorter events, 0.1 us)
Async XLA Ops:
  4.4 5.3 %collective-permute-start = (bf16[4,3,32,2048]{3,2,1,0:T(8,128)(2,1)S(1)}, bf16[4,3,32,2048]{3,2,1,0:T(8,128)(2,1)S(1)}, u32[]{:S(2)}, u32[]{:S(2)}) collective-permute-start(bf16[4,3,32,2048]{3,2,1,0:T(8,128)(2,1)S(1)} %dynamic-slice_bitcast_fusion), channel_id=1, source_target_pairs={{0,32},{32,0},{64,96},{96,64},{128,160},{160,128},{192,224},{224,1... | collective-permute-start | bytes 4718600 | tf_op jit(solution)/shard_map/ppermute | solution.py:86
  9.9 52.2 %copy-start = (s32[32]{0:T(128)S(1)}, s32[32]{0:T(128)}, u32[]{:S(2)}) copy-start(s32[32]{0:T(128)} %param.5) | copy-start | bytes 388
  9.9 26.8 %collective-permute-start.1 = (bf16[4,32,2048]{2,1,0:T(8,128)(2,1)S(1)}, bf16[4,32,2048]{2,1,0:T(8,128)(2,1)S(1)}, u32[]{:S(2)}, u32[]{:S(2)}) collective-permute-start(bf16[4,32,2048]{2,1,0:T(8,128)(2,1)S(1)} %get-tuple-element.8), channel_id=1, source_target_pairs={{0,64},{32,96},{64,128},{96,160},{128,192},{160,224},{192,256},{22... | collective-permute-start | bytes 1572872 | tf_op jit(solution)/shard_map/ppermute | solution.py:96
  14.2 59.1 %copy-start.1 = (f32[1,32,1,2048]{3,2,1,0:T(1,128)S(1)}, f32[1,32,1,2048]{3,2,1,0:T(1,128)}, u32[]{:S(2)}) copy-start(f32[1,32,1,2048]{3,2,1,0:T(1,128)} %param.4) | copy-start | bytes 786436
  14.2 23.8 %collective-permute-start.2 = (bf16[4,32,2048]{2,1,0:T(8,128)(2,1)S(1)}, bf16[4,32,2048]{2,1,0:T(8,128)(2,1)S(1)}, u32[]{:S(2)}, u32[]{:S(2)}) collective-permute-start(bf16[4,32,2048]{2,1,0:T(8,128)(2,1)S(1)} %get-tuple-element.9), channel_id=1, source_target_pairs={{0,704},{32,736},{64,0},{96,32},{128,64},{160,96},{192,128},{224,1... | collective-permute-start | bytes 1572872 | tf_op jit(solution)/shard_map/ppermute | solution.py:97
  38.3 15.6 %collective-permute-start.3 = (bf16[32,2048]{1,0:T(8,128)(2,1)S(1)}, bf16[32,2048]{1,0:T(8,128)(2,1)S(1)}, u32[]{:S(2)}, u32[]{:S(2)}) collective-permute-start(bf16[32,2048]{1,0:T(8,128)(2,1)S(1)} %get-tuple-element.11), channel_id=1, source_target_pairs={{0,192},{32,224},{64,256},{96,288},{128,320},{160,352},{192,384},{... | collective-permute-start | bytes 393224 | tf_op jit(solution)/shard_map/ppermute | solution.py:108
  40.5 20.8 %collective-permute-start.4 = (bf16[32,2048]{1,0:T(8,128)(2,1)S(1)}, bf16[32,2048]{1,0:T(8,128)(2,1)S(1)}, u32[]{:S(2)}, u32[]{:S(2)}) collective-permute-start(bf16[32,2048]{1,0:T(8,128)(2,1)S(1)} %get-tuple-element.12), channel_id=1, source_target_pairs={{0,576},{32,608},{64,640},{96,672},{128,704},{160,736},{192,0},{22... | collective-permute-start | bytes 393224 | tf_op jit(solution)/shard_map/ppermute | solution.py:108
  47.2 14.9 %collective-permute-start.5 = (bf16[32,2048]{1,0:T(8,128)(2,1)S(1)}, bf16[32,2048]{1,0:T(8,128)(2,1)S(1)}, u32[]{:S(2)}, u32[]{:S(2)}) collective-permute-start(bf16[32,2048]{1,0:T(8,128)(2,1)S(1)} %get-tuple-element.13), channel_id=1, source_target_pairs={{0,384},{32,416},{64,448},{96,480},{128,512},{160,544},{192,576},{... | collective-permute-start | bytes 393224 | tf_op jit(solution)/shard_map/ppermute | solution.py:108
  63.2 21.2 %all-to-all-start = ((f32[32,16,128]{2,1,0:T(8,128)}), f32[32,16,128]{2,1,0:T(8,128)S(1)}, u32[]{:S(2)}, u32[]{:S(2)}) async-start(f32[32,16,128]{2,1,0:T(8,128)} %place.1), calls=%async_computation | async-start | bytes 524288 | tf_op jit(solution)/shard_map/all_to_all | solution.py:189
  108.5 12.7 %collective-permute-start.7 = (bf16[128,2048]{1,0:T(8,128)(2,1)S(1)}, bf16[128,2048]{1,0:T(8,128)(2,1)S(1)}, u32[]{:S(2)}, u32[]{:S(2)}) collective-permute-start(bf16[128,2048]{1,0:T(8,128)(2,1)S(1)} %all_gather.3.refs_1_), channel_id=1, source_target_pairs={{0,704},{32,736},{64,0},{96,32},{128,64},{160,96},{192,128},{224,1... | collective-permute-start | bytes 1572872 | tf_op jit(solution)/shard_map/ppermute | solution.py:122
  114.5 12.3 %collective-permute-start.6 = (bf16[128,2048]{1,0:T(8,128)(2,1)S(1)}, bf16[128,2048]{1,0:T(8,128)(2,1)S(1)}, u32[]{:S(2)}, u32[]{:S(2)}) collective-permute-start(bf16[128,2048]{1,0:T(8,128)(2,1)S(1)} %all_gather.3.refs_1_), channel_id=1, source_target_pairs={{0,64},{32,96},{64,128},{96,160},{128,192},{160,224},{192,256},{22... | collective-permute-start | bytes 1572872 | tf_op jit(solution)/shard_map/ppermute | solution.py:121
  116.5 12.3 %collective-permute-start.8 = (bf16[128,2048]{1,0:T(8,128)(2,1)S(1)}, bf16[128,2048]{1,0:T(8,128)(2,1)S(1)}, u32[]{:S(2)}, u32[]{:S(2)}) collective-permute-start(bf16[128,2048]{1,0:T(8,128)(2,1)S(1)} %all_gather.3.refs_1_), channel_id=1, source_target_pairs={{0,32},{32,0},{64,96},{96,64},{128,160},{160,128},{192,224},{224,1... | collective-permute-start | bytes 1572872 | tf_op jit(solution)/shard_map/ppermute | solution.py:124
  121.2 7.6 %collective-permute-start.10 = (bf16[128,2048]{1,0:T(8,128)(2,1)S(1)}, bf16[128,2048]{1,0:T(8,128)(2,1)S(1)}, u32[]{:S(2)}, u32[]{:S(2)}) collective-permute-start(bf16[128,2048]{1,0:T(8,128)(2,1)S(1)} %collective-permute-done.7.refs_3_), channel_id=1, source_target_pairs={{0,32},{32,0},{64,96},{96,64},{128,160},{160,128},{192,224},{224,1... | collective-permute-start | bytes 1572872 | tf_op jit(solution)/shard_map/ppermute | solution.py:124
  126.8 3.8 %collective-permute-start.9 = (bf16[128,2048]{1,0:T(8,128)(2,1)S(1)}, bf16[128,2048]{1,0:T(8,128)(2,1)S(1)}, u32[]{:S(2)}, u32[]{:S(2)}) collective-permute-start(bf16[128,2048]{1,0:T(8,128)(2,1)S(1)} %collective-permute-done.6.refs_2_), channel_id=1, source_target_pairs={{0,32},{32,0},{64,96},{96,64},{128,160},{160,128},{192,224},{224,1... | collective-permute-start | bytes 1572872 | tf_op jit(solution)/shard_map/ppermute | solution.py:124

commit v3 on v2

--- a/solution.py
+++ b/solution.py
@@ -56,29 +56,32 @@
             out_ref[n] = (mine_ref[n, there, core].astype(F32) + theirs_ref[n, there].astype(F32)).astype(BF16)
 
 
-def cluster_sums_kernel(replica_ref, mine_ref, theirs_ref, below_ref, above_ref, *out_refs):
+def cluster_sums_kernel(replica_ref, owner_ref, mine_ref, theirs_ref, below_ref, above_ref, out_ref, row_ref):
     core = lax.rem(replica_ref[0], 2)
-    chip = lax.div(replica_ref[0], 2)
-    kind, place = lax.rem(chip, STRIDE), lax.div(chip, STRIDE)
-    for step, out_ref in enumerate(out_refs):
-        n = lax.rem(place + step, len(out_refs))
+    kind = lax.rem(lax.div(replica_ref[0], 2), STRIDE)
+    experts, tiles, lanes = row_ref.shape
+    for n in range(out_ref.shape[0]):
         total = mine_ref[n, kind, core].astype(F32) + theirs_ref[n, kind].astype(F32)
-        out_ref[...] = (total + below_ref[n].astype(F32) + above_ref[n].astype(F32)).astype(BF16)
-
-
-def place_kernel(owner_ref, *refs):
-    parts, out_ref = refs[:-1], refs[-1]
-    slots, tiles, lanes = out_ref.shape
-    slot = lax.broadcasted_iota(jnp.int32, (slots, slots), 0)
-    onehot = jnp.where(slot == owner_ref[...], 1.0, 0.0).astype(BF16)
-    total = product(onehot, parts[0][...])
-    for part in parts[1:]:
-        total += product(onehot, part[...])
+        total += below_ref[n].astype(F32) + above_ref[n].astype(F32)
+        for tile in range(tiles):
+            row_ref[:, tile, :] = total[:, tile * lanes : (tile + 1) * lanes]
+        for expert in range(experts):
+            out_ref[n, owner_ref[expert]] = row_ref[expert].astype(BF16)
+
+
+def momentum_kernel(terms_ref, moment_ref, moment_out_ref, rows_ref, row_ref):
+    total = terms_ref[0].astype(F32)
+    for n in range(1, terms_ref.shape[0]):
+        total += terms_ref[n].astype(F32)
+    moment = DECAY_RATE * moment_ref[...] + total
+    moment_out_ref[...] = moment
+    row_ref[...] = total + DECAY_RATE * moment
+    _, tiles, lanes = row_ref.shape
     for tile in range(tiles):
-        out_ref[:, tile, :] = total[:, tile * lanes : (tile + 1) * lanes]
-
-
-def sum_rows(grads, owner, replica, replicas, lanes):
+        rows_ref[:, tile * lanes : (tile + 1) * lanes] = row_ref[:, tile, :].astype(BF16)
+
+
+def cluster_sums(grads, owner, replica, replicas, lanes):
     experts, _, width = grads.shape
     members = replicas // (2 * STRIDE)
     here = replica.reshape(1)
@@ -95,25 +98,29 @@
     )(here, mine, theirs)
     below = lax.ppermute(up, "rep", shift(1, replicas))
     above = lax.ppermute(down, "rep", shift(-1, replicas))
-    sums = pl.pallas_call(
+    tiles = (experts, width // lanes, lanes)
+    return pl.pallas_call(
         cluster_sums_kernel,
-        out_shape=(jax.ShapeDtypeStruct((experts, width), BF16),) * members,
-        in_specs=[SCALARS] + [VECTORS] * 4,
-        out_specs=(VECTORS,) * members,
+        out_shape=jax.ShapeDtypeStruct((members, *tiles), BF16),
+        in_specs=[SCALARS] * 2 + [VECTORS] * 4,
+        out_specs=VECTORS,
+        scratch_shapes=[pltpu.VMEM(tiles, F32)],
         compiler_params=grant(12),
         name="cluster_sums",
-    )(here, mine, theirs, below, above)
-    parts = [sums[0]]
-    for step in sorted(range(1, members), key=lambda n: abs(2 * n - members), reverse=True):
-        parts.append(lax.ppermute(sums[step], "rep", shift(STRIDE * step, replicas)))
+    )(here, owner, mine, theirs, below, above)
+
+
+def momentum_rows(terms, moment):
+    slots, tiles, lanes = moment.shape
     return pl.pallas_call(
-        place_kernel,
-        out_shape=jax.ShapeDtypeStruct((experts, width // lanes, lanes), F32),
-        in_specs=[VECTORS] * (1 + members),
-        out_specs=VECTORS,
+        momentum_kernel,
+        out_shape=(jax.ShapeDtypeStruct(moment.shape, F32), jax.ShapeDtypeStruct((slots, tiles * lanes), BF16)),
+        in_specs=[VECTORS, VECTORS],
+        out_specs=(VECTORS, VECTORS),
+        scratch_shapes=[pltpu.VMEM(moment.shape, F32)],
         compiler_params=grant(4),
-        name="place",
-    )(owner.reshape(1, -1), *parts)
+        name="momentum",
+    )(terms, moment)
 
 
 def gather_rows(rows, replicas):
@@ -185,10 +192,13 @@
     lanes = math.gcd(width, 128)
     tiled = (slots, width // lanes, lanes)
 
-    outgoing = sum_rows(grads[0], owner, replica, replicas, lanes)
-    grad_rows = lax.all_to_all(outgoing, "fsdp", split_axis=0, concat_axis=0, tiled=True)
-    moment_new = DECAY_RATE * momentum.reshape(tiled) + grad_rows
-    nesterov = (grad_rows + DECAY_RATE * moment_new).astype(BF16).reshape(slots, width)
+    sums = cluster_sums(grads[0], owner, replica, replicas, lanes)
+    members = sums.shape[0]
+    groups = [[r * slots + s for r in group for s in range(slots)] for group in classes(replicas)]
+    terms = lax.all_to_all(
+        sums.reshape(members * slots, *tiled[1:]), ("rep", "fsdp"), 0, 0, axis_index_groups=groups, tiled=True
+    )
+    moment_new, nesterov = momentum_rows(terms.reshape(members, *tiled), momentum.reshape(tiled))
 
     pieces = gather_rows(nesterov, replicas)
     update_rows = newton_rows(pieces, slots, (replica // (2 * STRIDE)) * slots, math.sqrt(width))

time: 154 us -> 149 us (0.968)
  blocking collectives: 38 us -> 79.9 us
  starting transfers between devices: 58 us -> 32 us
  waiting for transfers between devices: 42.1 us -> 20.7 us
    all_to_all x0 -> x1, blocking collectives: none -> 42.8 us  [on_device(): lax.all_to_all(sums.reshape(members * slots, *tiled[1:]), ('rep', 'fsdp')...]
    ppermute x6 -> x3, starting transfers between devices: 34.1 us -> 18.6 us  [the longest x1 12.4 us: cluster_sums(): above = lax.ppermute(down, 'rep', shift(-1, replicas))]
    all_to_all x1 -> x0, waiting for transfers between devices: 10.8 us -> none  [on_device(): lax.all_to_all(outgoing, 'fsdp', split_axis=0, concat_axis=0, tiled=True)]
    all_to_all x1 -> x0, starting transfers between devices: 10.2 us -> none  [on_device(): lax.all_to_all(outgoing, 'fsdp', split_axis=0, concat_axis=0, tiled=True)]
    ppermute x6 -> x3, waiting for transfers between devices: 23 us -> 14.8 us  [the longest x1 10.1 us: cluster_sums(): below = lax.ppermute(up, 'rep', shift(1, replicas))]
    all_gather x1, blocking collectives: 23.3 us -> 18.2 us  [gather_rows(): lax.all_gather(rows, 'rep', axis=0, tiled=True, axis_index_groups=classes...]
    all_to_all x1, blocking collectives: 14.7 us -> 18.9 us  [on_device(): lax.all_to_all(update_rows.reshape(tiled), 'fsdp', split_axis=0, concat_a...]
    ppermute x1, waiting for transfers between devices: 2.82 us -> 0.94 us  [gather_rows(): above = lax.ppermute(own, 'rep', shift(-1, replicas))]
  transfers between devices with their start and end apart: 12 -> 8, of which waited for: 9 -> 6; matrix products, arithmetic and copies ran while one was open for 0% -> 0% of each run, Pallas kernels for 0% -> 0%
where the time goes in v3:
time: 149 us; the launch traced here: 148 us
  blocking collectives  79.9 us (54%)
  starting transfers between devices  32 us (21%)
  waiting for transfers between devices  20.7 us (14%)
  Pallas kernels  10.1 us (7%)
  local copies, waits for them, and re-layouts  3.76 us (3%)
    all_to_all x1, blocking collectives, on_device(): lax.all_to_all(sums.reshape(members * slots, *tiled[1:]), ('rep', 'fsdp')...  42.8 us
    all_to_all x1, blocking collectives, on_device(): lax.all_to_all(update_rows.reshape(tiled), 'fsdp', split_axis=0, concat_a...  18.9 us
    all_gather x1, blocking collectives, gather_rows(): lax.all_gather(rows, 'rep', axis=0, tiled=True, axis_index_groups=classes...  18.2 us
    ppermute x1, starting transfers between devices, cluster_sums(): above = lax.ppermute(down, 'rep', shift(-1, replicas))  12.4 us
    ppermute x1, waiting for transfers between devices, cluster_sums(): below = lax.ppermute(up, 'rep', shift(1, replicas))  10.1 us
    pallas_call x1, Pallas kernels, newton_rows(): pl.pallas_call(lambda *refs: newton_kernel(count, factor, *refs), out_sha...  7.49 us
    ppermute x3, starting transfers between devices, gather_rows(): lax.ppermute(piece, 'rep', other_core(replicas))  5.92 us
    ppermute x1, starting transfers between devices, gather_rows(): above = lax.ppermute(own, 'rep', shift(-1, replicas))  4.52 us
  transfers between devices with their start and end apart: 8, of which 6 were waited for; matrix products, arithmetic and copies ran while one was open for 0% of the time, Pallas kernels for 0%

profile of v3, /device:TPU:8, one launch (start us, length us, event | category | flops | bytes accessed | tf_op | source)
XLA Modules:
  0.0 148.2 jit_solution(5550573540227235098)
XLA Ops:
  0.6 3.6 %copy.5 = bf16[24,32,2048]{2,1,0:T(8,128)(2,1)S(1)} copy(bf16[24,32,2048]{2,0,1:T(8,128)(2,1)} %bitcast.27) | data formatting | bytes 6291456 | tf_op jit(solution)/shard_map/transpose | solution.py:88
  4.3 0.1 dynamic-slice_bitcast_fusion
  4.4 0.0 copy-start.1
  4.4 1.9 %collective-permute-start = (bf16[4,3,32,2048]{3,2,1,0:T(8,128)(2,1)S(1)}, bf16[4,3,32,2048]{3,2,1,0:T(8,128)(2,1)S(1)}, u32[]{:S(2)}, u32[]{:S(2)}) collective-permute-start(bf16[4,3,32,2048]{3,2,1,0:T(8,128)(2,1)S(1)} %dynamic-slice_bitcast_fusion), channel_id=1, source_target_pairs={{0,32},{32,0},{64,96},{96,64},{128,160},{160,128},{192,224},{224,1... | collective-permute-start | bytes 4718600 | tf_op jit(solution)/shard_map/ppermute | solution.py:89
  6.3 3.4 %collective-permute-done.theirs_ref = bf16[4,3,32,2048]{3,2,1,0:T(8,128)(2,1)S(1)} collective-permute-done((bf16[4,3,32,2048]{3,2,1,0:T(8,128)(2,1)S(1)}, bf16[4,3,32,2048]{3,2,1,0:T(8,128)(2,1)S(1)}, u32[]{:S(2)}, u32[]{:S(2)}) %collective-permute-start) | collective-permute-done | bytes 1572896 | tf_op jit(solution)/shard_map/ppermute | solution.py:89
  9.7 0.2 chip_sums.1
  9.9 4.3 %collective-permute-start.1 = (bf16[4,32,2048]{2,1,0:T(8,128)(2,1)S(1)}, bf16[4,32,2048]{2,1,0:T(8,128)(2,1)S(1)}, u32[]{:S(2)}, u32[]{:S(2)}) collective-permute-start(bf16[4,32,2048]{2,1,0:T(8,128)(2,1)S(1)} %get-tuple-element.6), channel_id=1, source_target_pairs={{0,64},{32,96},{64,128},{96,160},{128,192},{160,224},{192,256},{22... | collective-permute-start | bytes 1572872 | tf_op jit(solution)/shard_map/ppermute | solution.py:99
  14.2 0.0 copy-start
  14.2 12.4 %collective-permute-start.2 = (bf16[4,32,2048]{2,1,0:T(8,128)(2,1)S(1)}, bf16[4,32,2048]{2,1,0:T(8,128)(2,1)S(1)}, u32[]{:S(2)}, u32[]{:S(2)}) collective-permute-start(bf16[4,32,2048]{2,1,0:T(8,128)(2,1)S(1)} %get-tuple-element.7), channel_id=1, source_target_pairs={{0,704},{32,736},{64,0},{96,32},{128,64},{160,96},{192,128},{224,1... | collective-permute-start | bytes 1572872 | tf_op jit(solution)/shard_map/ppermute | solution.py:100
  26.6 10.1 %collective-permute-done.1.below_ref = bf16[4,32,2048]{2,1,0:T(8,128)(2,1)S(1)} collective-permute-done((bf16[4,32,2048]{2,1,0:T(8,128)(2,1)S(1)}, bf16[4,32,2048]{2,1,0:T(8,128)(2,1)S(1)}, u32[]{:S(2)}, u32[]{:S(2)}) %collective-permute-start.1) | collective-permute-done | bytes 524320 | tf_op jit(solution)/shard_map/ppermute | solution.py:99
  36.8 1.3 collective-permute-done.2.above_ref
  38.1 0.0 copy-done.1
  38.1 1.5 %cluster_sums.1 = bf16[4,32,16,128]{3,2,1,0:T(8,128)(2,1)S(1)} custom-call(s32[1]{0:T(128)} %bitcast.1.replica_ref, s32[32]{0:T(128)S(1)} %copy-done.1, bf16[4,3,2,32,2048]{4,3,2,1,0:T(8,128)(2,1)S(1)} %bitcast.22, bf16[4,3,32,2048]{3,2,1,0:T(8,128)(2,1)S(1)} %collective-permute-done.theirs_ref, bf16[4,32,2048]{2,1,0:T(8,128)(2,1)S(1)} %collective-permute-done.1.below_ref, ...), custom_call_target="tpu_custom_call" | custom-call | tf_op jit(solution)/shard_map/cluster_sums/pallas_call | solution.py:102
  39.6 42.8 %all_to_all.10 = bf16[128,16,128]{2,1,0:T(8,128)(2,1)S(1)} all-to-all(bf16[128,16,128]{2,1,0:T(8,128)(2,1)S(1)} %bitcast.24), channel_id=1, replica_groups={{0,1,2,3,4,5,6,7,8,9,10,11,12,13,14,15,16,17,18,19,20,21,22,23,24,25,26..., dimensions={0} | all-to-all | bytes 1048576 | tf_op jit(solution)/shard_map/all_to_all | solution.py:198
  82.4 0.0 copy-done
  82.4 0.8 momentum.1
  83.2 18.2 %all_gather.3.refs_1_ = bf16[128,2048]{1,0:T(8,128)(2,1)S(1)} all-gather(bf16[32,2048]{1,0:T(8,128)(2,1)S(1)} %get-tuple-element.8), channel_id=1, replica_groups={{0,192,384,576},{32,224,416,608},{64,256,448,640},{96,288,480,672},{128..., dimensions={0}, use_global_device_ids=true | all-gather | bytes 655360 | tf_op jit(solution)/shard_map/all_gather | solution.py:127
  101.4 3.0 %collective-permute-start.3 = (bf16[128,2048]{1,0:T(8,128)(2,1)S(1)}, bf16[128,2048]{1,0:T(8,128)(2,1)S(1)}, u32[]{:S(2)}, u32[]{:S(2)}) collective-permute-start(bf16[128,2048]{1,0:T(8,128)(2,1)S(1)} %all_gather.3.refs_1_), channel_id=1, source_target_pairs={{0,64},{32,96},{64,128},{96,160},{128,192},{160,224},{192,256},{22... | collective-permute-start | bytes 1572872 | tf_op jit(solution)/shard_map/ppermute | solution.py:128
  104.4 4.5 %collective-permute-start.4 = (bf16[128,2048]{1,0:T(8,128)(2,1)S(1)}, bf16[128,2048]{1,0:T(8,128)(2,1)S(1)}, u32[]{:S(2)}, u32[]{:S(2)}) collective-permute-start(bf16[128,2048]{1,0:T(8,128)(2,1)S(1)} %all_gather.3.refs_1_), channel_id=1, source_target_pairs={{0,704},{32,736},{64,0},{96,32},{128,64},{160,96},{192,128},{224,1... | collective-permute-start | bytes 1572872 | tf_op jit(solution)/shard_map/ppermute | solution.py:129
  109.0 1.9 %collective-permute-start.5 = (bf16[128,2048]{1,0:T(8,128)(2,1)S(1)}, bf16[128,2048]{1,0:T(8,128)(2,1)S(1)}, u32[]{:S(2)}, u32[]{:S(2)}) collective-permute-start(bf16[128,2048]{1,0:T(8,128)(2,1)S(1)} %all_gather.3.refs_1_), channel_id=1, source_target_pairs={{0,32},{32,0},{64,96},{96,64},{128,160},{160,128},{192,224},{224,1... | collective-permute-start | bytes 1572872 | tf_op jit(solution)/shard_map/ppermute | solution.py:131
  110.9 3.3 %collective-permute-done.3.refs_2_ = bf16[128,2048]{1,0:T(8,128)(2,1)S(1)} collective-permute-done((bf16[128,2048]{1,0:T(8,128)(2,1)S(1)}, bf16[128,2048]{1,0:T(8,128)(2,1)S(1)}, u32[]{:S(2)}, u32[]{:S(2)}) %collective-permute-start.3) | collective-permute-done | bytes 524320 | tf_op jit(solution)/shard_map/ppermute | solution.py:128
  114.2 1.9 %collective-permute-start.6 = (bf16[128,2048]{1,0:T(8,128)(2,1)S(1)}, bf16[128,2048]{1,0:T(8,128)(2,1)S(1)}, u32[]{:S(2)}, u32[]{:S(2)}) collective-permute-start(bf16[128,2048]{1,0:T(8,128)(2,1)S(1)} %collective-permute-done.3.refs_2_), channel_id=1, source_target_pairs={{0,32},{32,0},{64,96},{96,64},{128,160},{160,128},{192,224},{224,1... | collective-permute-start | bytes 1572872 | tf_op jit(solution)/shard_map/ppermute | solution.py:131
  116.1 0.9 collective-permute-done.4.refs_3_
  117.1 2.1 %collective-permute-start.7 = (bf16[128,2048]{1,0:T(8,128)(2,1)S(1)}, bf16[128,2048]{1,0:T(8,128)(2,1)S(1)}, u32[]{:S(2)}, u32[]{:S(2)}) collective-permute-start(bf16[128,2048]{1,0:T(8,128)(2,1)S(1)} %collective-permute-done.4.refs_3_), channel_id=1, source_target_pairs={{0,32},{32,0},{64,96},{96,64},{128,160},{160,128},{192,224},{224,1... | collective-permute-start | bytes 1572872 | tf_op jit(solution)/shard_map/ppermute | solution.py:131
  119.2 0.0 collective-permute-done.5.refs_4_
  119.2 0.0 collective-permute-done.6.refs_5_
  119.2 1.7 %collective-permute-done.7.refs_6_ = bf16[128,2048]{1,0:T(8,128)(2,1)S(1)} collective-permute-done((bf16[128,2048]{1,0:T(8,128)(2,1)S(1)}, bf16[128,2048]{1,0:T(8,128)(2,1)S(1)}, u32[]{:S(2)}, u32[]{:S(2)}) %collective-permute-start.7) | collective-permute-done | bytes 524320 | tf_op jit(solution)/shard_map/ppermute | solution.py:131
  120.8 7.5 %newton.1 = bf16[32,2048]{1,0:T(8,128)(2,1)S(1)} custom-call(s32[1]{0:T(128)} %bitcast.refs_0_, bf16[128,2048]{1,0:T(8,128)(2,1)S(1)} %all_gather.3.refs_1_, bf16[128,2048]{1,0:T(8,128)(2,1)S(1)} %collective-permute-done.3.refs_2_, bf16[128,2048]{1,0:T(8,128)(2,1)S(1)} %collective-permute-done.4.refs_3_, ...), custom_call_target="tpu_custom_call" | custom-call | tf_op jit(solution)/shard_map/newton/pallas_call | solution.py:176
  128.4 18.9 %all_to_all.11 = bf16[32,16,128]{2,1,0:T(8,128)(2,1)S(1)} all-to-all(bf16[32,16,128]{2,1,0:T(8,128)(2,1)S(1)} %bitcast.28), channel_id=1, replica_groups=mesh['rep'=24,'fsdp'=32] {'fsdp'}, dimensions={0} | all-to-all | bytes 262144 | tf_op jit(solution)/shard_map/all_to_all | solution.py:206
  147.3 0.9 fusion
  (1 shorter events, 0.0 us)
Async XLA Ops:
  4.4 33.7 %copy-start.1 = (s32[32]{0:T(128)S(1)}, s32[32]{0:T(128)}, u32[]{:S(2)}) copy-start(s32[32]{0:T(128)} %owner_ref.1) | copy-start | bytes 388
  4.4 5.3 %collective-permute-start = (bf16[4,3,32,2048]{3,2,1,0:T(8,128)(2,1)S(1)}, bf16[4,3,32,2048]{3,2,1,0:T(8,128)(2,1)S(1)}, u32[]{:S(2)}, u32[]{:S(2)}) collective-permute-start(bf16[4,3,32,2048]{3,2,1,0:T(8,128)(2,1)S(1)} %dynamic-slice_bitcast_fusion), channel_id=1, source_target_pairs={{0,32},{32,0},{64,96},{96,64},{128,160},{160,128},{192,224},{224,1... | collective-permute-start | bytes 4718600 | tf_op jit(solution)/shard_map/ppermute | solution.py:89
  9.9 26.8 %collective-permute-start.1 = (bf16[4,32,2048]{2,1,0:T(8,128)(2,1)S(1)}, bf16[4,32,2048]{2,1,0:T(8,128)(2,1)S(1)}, u32[]{:S(2)}, u32[]{:S(2)}) collective-permute-start(bf16[4,32,2048]{2,1,0:T(8,128)(2,1)S(1)} %get-tuple-element.6), channel_id=1, source_target_pairs={{0,64},{32,96},{64,128},{96,160},{128,192},{160,224},{192,256},{22... | collective-permute-start | bytes 1572872 | tf_op jit(solution)/shard_map/ppermute | solution.py:99
  14.2 68.2 %copy-start = (f32[1,32,1,2048]{3,2,1,0:T(1,128)S(1)}, f32[1,32,1,2048]{3,2,1,0:T(1,128)}, u32[]{:S(2)}) copy-start(f32[1,32,1,2048]{3,2,1,0:T(1,128)} %param.4) | copy-start | bytes 786436
  14.2 23.8 %collective-permute-start.2 = (bf16[4,32,2048]{2,1,0:T(8,128)(2,1)S(1)}, bf16[4,32,2048]{2,1,0:T(8,128)(2,1)S(1)}, u32[]{:S(2)}, u32[]{:S(2)}) collective-permute-start(bf16[4,32,2048]{2,1,0:T(8,128)(2,1)S(1)} %get-tuple-element.7), channel_id=1, source_target_pairs={{0,704},{32,736},{64,0},{96,32},{128,64},{160,96},{192,128},{224,1... | collective-permute-start | bytes 1572872 | tf_op jit(solution)/shard_map/ppermute | solution.py:100
  101.4 12.8 %collective-permute-start.3 = (bf16[128,2048]{1,0:T(8,128)(2,1)S(1)}, bf16[128,2048]{1,0:T(8,128)(2,1)S(1)}, u32[]{:S(2)}, u32[]{:S(2)}) collective-permute-start(bf16[128,2048]{1,0:T(8,128)(2,1)S(1)} %all_gather.3.refs_1_), channel_id=1, source_target_pairs={{0,64},{32,96},{64,128},{96,160},{128,192},{160,224},{192,256},{22... | collective-permute-start | bytes 1572872 | tf_op jit(solution)/shard_map/ppermute | solution.py:128
  104.4 12.6 %collective-permute-start.4 = (bf16[128,2048]{1,0:T(8,128)(2,1)S(1)}, bf16[128,2048]{1,0:T(8,128)(2,1)S(1)}, u32[]{:S(2)}, u32[]{:S(2)}) collective-permute-start(bf16[128,2048]{1,0:T(8,128)(2,1)S(1)} %all_gather.3.refs_1_), channel_id=1, source_target_pairs={{0,704},{32,736},{64,0},{96,32},{128,64},{160,96},{192,128},{224,1... | collective-permute-start | bytes 1572872 | tf_op jit(solution)/shard_map/ppermute | solution.py:129
  109.0 10.2 %collective-permute-start.5 = (bf16[128,2048]{1,0:T(8,128)(2,1)S(1)}, bf16[128,2048]{1,0:T(8,128)(2,1)S(1)}, u32[]{:S(2)}, u32[]{:S(2)}) collective-permute-start(bf16[128,2048]{1,0:T(8,128)(2,1)S(1)} %all_gather.3.refs_1_), channel_id=1, source_target_pairs={{0,32},{32,0},{64,96},{96,64},{128,160},{160,128},{192,224},{224,1... | collective-permute-start | bytes 1572872 | tf_op jit(solution)/shard_map/ppermute | solution.py:131
  114.2 5.0 %collective-permute-start.6 = (bf16[128,2048]{1,0:T(8,128)(2,1)S(1)}, bf16[128,2048]{1,0:T(8,128)(2,1)S(1)}, u32[]{:S(2)}, u32[]{:S(2)}) collective-permute-start(bf16[128,2048]{1,0:T(8,128)(2,1)S(1)} %collective-permute-done.3.refs_2_), channel_id=1, source_target_pairs={{0,32},{32,0},{64,96},{96,64},{128,160},{160,128},{192,224},{224,1... | collective-permute-start | bytes 1572872 | tf_op jit(solution)/shard_map/ppermute | solution.py:131
  117.1 3.8 %collective-permute-start.7 = (bf16[128,2048]{1,0:T(8,128)(2,1)S(1)}, bf16[128,2048]{1,0:T(8,128)(2,1)S(1)}, u32[]{:S(2)}, u32[]{:S(2)}) collective-permute-start(bf16[128,2048]{1,0:T(8,128)(2,1)S(1)} %collective-permute-done.4.refs_3_), channel_id=1, source_target_pairs={{0,32},{32,0},{64,96},{96,64},{128,160},{160,128},{192,224},{224,1... | collective-permute-start | bytes 1572872 | tf_op jit(solution)/shard_map/ppermute | solution.py:131

commit v4 on v3

--- a/solution.py
+++ b/solution.py
@@ -26,8 +26,8 @@
     return pltpu.CompilerParams(vmem_limit_bytes=mebibytes * 2**20)
 
 
-def shift(chips, replicas):
-    return [(r, (r + 2 * chips) % replicas) for r in range(replicas)]
+def neighbours(turn, replicas):
+    return [(r, (r + 2 - 4 * ((r + turn) % 2)) % replicas) for r in range(replicas)]
 
 
 def other_core(replicas):
@@ -47,22 +47,22 @@
     return lax.dynamic_index_in_dim(array, index, axis, keepdims=False)
 
 
-def chip_sums_kernel(replica_ref, mine_ref, theirs_ref, up_ref, down_ref):
+def chip_sums_kernel(replica_ref, mine_ref, theirs_ref, *out_refs):
     core = lax.rem(replica_ref[0], 2)
     kind = lax.rem(lax.div(replica_ref[0], 2), STRIDE)
-    for step, out_ref in ((1, up_ref), (2, down_ref)):
+    for step, out_ref in zip((1 + core, 2 - core), out_refs, strict=True):
         there = lax.rem(kind + step, STRIDE)
         for n in range(out_ref.shape[0]):
             out_ref[n] = (mine_ref[n, there, core].astype(F32) + theirs_ref[n, there].astype(F32)).astype(BF16)
 
 
-def cluster_sums_kernel(replica_ref, owner_ref, mine_ref, theirs_ref, below_ref, above_ref, out_ref, row_ref):
+def cluster_sums_kernel(replica_ref, owner_ref, mine_ref, theirs_ref, first_ref, second_ref, out_ref, row_ref):
     core = lax.rem(replica_ref[0], 2)
     kind = lax.rem(lax.div(replica_ref[0], 2), STRIDE)
     experts, tiles, lanes = row_ref.shape
     for n in range(out_ref.shape[0]):
         total = mine_ref[n, kind, core].astype(F32) + theirs_ref[n, kind].astype(F32)
-        total += below_ref[n].astype(F32) + above_ref[n].astype(F32)
+        total += first_ref[n].astype(F32) + second_ref[n].astype(F32)
         for tile in range(tiles):
             row_ref[:, tile, :] = total[:, tile * lanes : (tile + 1) * lanes]
         for expert in range(experts):
@@ -88,7 +88,7 @@
     mine = grads.transpose(1, 0, 2).reshape(members, STRIDE, 2, experts, width)
     theirs = lax.ppermute(pick(mine, 1 - replica % 2, 2), "rep", other_core(replicas))
     some = jax.ShapeDtypeStruct((members, experts, width), BF16)
-    up, down = pl.pallas_call(
+    outward = pl.pallas_call(
         chip_sums_kernel,
         out_shape=(some, some),
         in_specs=[SCALARS, VECTORS, VECTORS],
@@ -96,8 +96,7 @@
         compiler_params=grant(12),
         name="chip_sums",
     )(here, mine, theirs)
-    below = lax.ppermute(up, "rep", shift(1, replicas))
-    above = lax.ppermute(down, "rep", shift(-1, replicas))
+    inward = [lax.ppermute(sums, "rep", neighbours(turn, replicas)) for turn, sums in enumerate(outward)]
     tiles = (experts, width // lanes, lanes)
     return pl.pallas_call(
         cluster_sums_kernel,
@@ -107,7 +106,7 @@
         scratch_shapes=[pltpu.VMEM(tiles, F32)],
         compiler_params=grant(12),
         name="cluster_sums",
-    )(here, owner, mine, theirs, below, above)
+    )(here, owner, mine, theirs, *inward)
 
 
 def momentum_rows(terms, moment):
@@ -125,9 +124,7 @@
 
 def gather_rows(rows, replicas):
     own = lax.all_gather(rows, "rep", axis=0, tiled=True, axis_index_groups=classes(replicas))
-    below = lax.ppermute(own, "rep", shift(1, replicas))
-    above = lax.ppermute(own, "rep", shift(-1, replicas))
-    pieces = [own, below, above]
+    pieces = [own] + [lax.ppermute(own, "rep", neighbours(turn, replicas)) for turn in range(2)]
     return pieces + [lax.ppermute(piece, "rep", other_core(replicas)) for piece in pieces]
 
 
@@ -136,7 +133,7 @@
 
 
 def newton_kernel(count, factor, first_ref, *refs):
-    pieces, (out_ref, x_ref, raw_ref, gram_ref, poly_ref, mixed_ref, next_ref) = refs[:-7], refs[-7:]
+    pieces, (out_ref, x_ref, raw_ref, gram_ref, poly_ref) = refs[:-5], refs[-5:]
     height = pieces[0].shape[0]
     for n, piece in enumerate(pieces):
         x_ref[pl.ds(n * height, height), :] = piece[...]
@@ -155,15 +152,16 @@
     for block in blocks:
         squared = product(gram_ref[block, :], gram_ref[...])
         poly_ref[block, :] = (NEWTON_B * gram_ref[block, :].astype(F32) + NEWTON_C * squared).astype(BF16)
-    for block in blocks:
-        mixed_ref[block, :] = product(gram_ref[block, :], poly_ref[...]).astype(BF16)
-    for block in blocks:
-        own = NEWTON_A * NEWTON_A * gram_ref[block, :].astype(F32) + 2.0 * NEWTON_A * mixed_ref[block, :].astype(F32)
-        next_ref[block, :] = (own + product(mixed_ref[block, :], poly_ref[...])).astype(BF16)
     rows = pl.ds(pl.multiple_of(first_ref[0], count), count)
-    own_gram = next_ref[rows, :]
-    own_poly = NEWTON_B * own_gram.astype(F32) + NEWTON_C * product(own_gram, next_ref[...])
-    own_poly = own_poly.astype(BF16)
+
+    def next_gram(before):
+        once = product(before.astype(BF16), poly_ref[...])
+        twice = product(once.astype(BF16), poly_ref[...])
+        return NEWTON_A * NEWTON_A * before + 2.0 * NEWTON_A * once + twice
+
+    own_gram = next_gram(gram_ref[rows, :].astype(F32)).astype(BF16)
+    squared = next_gram(product(own_gram, gram_ref[...]))
+    own_poly = (NEWTON_B * own_gram.astype(F32) + NEWTON_C * squared).astype(BF16)
     weights = NEWTON_A * (poly_ref[rows, :].astype(F32) + own_poly.astype(F32)) + product(own_poly, poly_ref[...])
     result = NEWTON_A * NEWTON_A * x_ref[rows, :].astype(F32) + product(weights.astype(BF16), x_ref[...])
     out_ref[...] = (factor * scale * result).astype(BF16)
@@ -178,7 +176,7 @@
         out_shape=jax.ShapeDtypeStruct((count, width), BF16),
         in_specs=[SCALARS] + [VECTORS] * len(pieces),
         out_specs=VECTORS,
-        scratch_shapes=[pltpu.VMEM((size, width), BF16), pltpu.VMEM((size, size), F32), square, square, square, square],
+        scratch_shapes=[pltpu.VMEM((size, width), BF16), pltpu.VMEM((size, size), F32), square, square],
         compiler_params=grant(20),
         name="newton",
     )(first_row.reshape(1), *pieces)

time: 149 us -> 149 us (level)
    all_to_all x1, blocking collectives: 18.9 us -> 16.8 us  [on_device(): lax.all_to_all(update_rows.reshape(tiled), 'fsdp', split_axis=0, concat_a...]
  transfers between devices with their start and end apart: 8 -> 8, of which waited for: 6 -> 5; matrix products, arithmetic and copies ran while one was open for 0% -> 0% of each run, Pallas kernels for 0% -> 0%
where the time goes in v4:
time: 149 us; the launch traced here: 148 us
  blocking collectives  79.9 us (54%)
  starting transfers between devices  32 us (21%)
  waiting for transfers between devices  21.4 us (14%)
  Pallas kernels  9.26 us (6%)
  local copies, waits for them, and re-layouts  3.76 us (3%)
    all_to_all x1, blocking collectives, on_device(): lax.all_to_all(sums.reshape(members * slots, *tiled[1:]), ('rep', 'fsdp')...  43.6 us
    all_gather x1, blocking collectives, gather_rows(): lax.all_gather(rows, 'rep', axis=0, tiled=True, axis_index_groups=classes...  19.5 us
    all_to_all x1, blocking collectives, on_device(): lax.all_to_all(update_rows.reshape(tiled), 'fsdp', split_axis=0, concat_a...  16.8 us
    ppermute x2, starting transfers between devices, cluster_sums(): lax.ppermute(sums, 'rep', neighbours(turn, replicas))  16.6 us
    ppermute x2, waiting for transfers between devices, cluster_sums(): lax.ppermute(sums, 'rep', neighbours(turn, replicas))  9.39 us
    ppermute x2, waiting for transfers between devices, gather_rows(): lax.ppermute(own, 'rep', neighbours(turn, replicas))  7.38 us
    ppermute x2, starting transfers between devices, gather_rows(): lax.ppermute(own, 'rep', neighbours(turn, replicas))  7.04 us
    pallas_call x1, Pallas kernels, newton_rows(): pl.pallas_call(lambda *refs: newton_kernel(count, factor, *refs), out_sha...  6.66 us
  transfers between devices with their start and end apart: 8, of which 5 were waited for; matrix products, arithmetic and copies ran while one was open for 0% of the time, Pallas kernels for 0%

profile of v4, /device:TPU:8, one launch (start us, length us, event | category | flops | bytes accessed | tf_op | source)
XLA Modules:
  0.0 148.1 jit_solution(12350355838656253507)
XLA Ops:
  0.6 3.6 %copy.5 = bf16[24,32,2048]{2,1,0:T(8,128)(2,1)S(1)} copy(bf16[24,32,2048]{2,0,1:T(8,128)(2,1)} %bitcast.27) | data formatting | bytes 6291456 | tf_op jit(solution)/shard_map/transpose | solution.py:88
  4.3 0.1 dynamic-slice_bitcast_fusion
  4.4 0.0 copy-start.1
  4.4 1.9 %collective-permute-start = (bf16[4,3,32,2048]{3,2,1,0:T(8,128)(2,1)S(1)}, bf16[4,3,32,2048]{3,2,1,0:T(8,128)(2,1)S(1)}, u32[]{:S(2)}, u32[]{:S(2)}) collective-permute-start(bf16[4,3,32,2048]{3,2,1,0:T(8,128)(2,1)S(1)} %dynamic-slice_bitcast_fusion), channel_id=1, source_target_pairs={{0,32},{32,0},{64,96},{96,64},{128,160},{160,128},{192,224},{224,1... | collective-permute-start | bytes 4718600 | tf_op jit(solution)/shard_map/ppermute | solution.py:89
  6.3 3.4 %collective-permute-done.theirs_ref = bf16[4,3,32,2048]{3,2,1,0:T(8,128)(2,1)S(1)} collective-permute-done((bf16[4,3,32,2048]{3,2,1,0:T(8,128)(2,1)S(1)}, bf16[4,3,32,2048]{3,2,1,0:T(8,128)(2,1)S(1)}, u32[]{:S(2)}, u32[]{:S(2)}) %collective-permute-start) | collective-permute-done | bytes 1572896 | tf_op jit(solution)/shard_map/ppermute | solution.py:89
  9.7 0.2 chip_sums.1
  9.9 4.3 %collective-permute-start.1 = (bf16[4,32,2048]{2,1,0:T(8,128)(2,1)S(1)}, bf16[4,32,2048]{2,1,0:T(8,128)(2,1)S(1)}, u32[]{:S(2)}, u32[]{:S(2)}) collective-permute-start(bf16[4,32,2048]{2,1,0:T(8,128)(2,1)S(1)} %get-tuple-element.6), channel_id=1, source_target_pairs={{0,64},{32,736},{64,128},{96,32},{128,192},{160,96},{192,256},{224... | collective-permute-start | bytes 1572872 | tf_op jit(solution)/shard_map/ppermute | solution.py:99
  14.2 0.0 copy-start
  14.2 12.4 %collective-permute-start.2 = (bf16[4,32,2048]{2,1,0:T(8,128)(2,1)S(1)}, bf16[4,32,2048]{2,1,0:T(8,128)(2,1)S(1)}, u32[]{:S(2)}, u32[]{:S(2)}) collective-permute-start(bf16[4,32,2048]{2,1,0:T(8,128)(2,1)S(1)} %get-tuple-element.7), channel_id=1, source_target_pairs={{0,704},{32,96},{64,0},{96,160},{128,64},{160,224},{192,128},{224,... | collective-permute-start | bytes 1572872 | tf_op jit(solution)/shard_map/ppermute | solution.py:99
  26.6 6.5 %collective-permute-done.1.first_ref = bf16[4,32,2048]{2,1,0:T(8,128)(2,1)S(1)} collective-permute-done((bf16[4,32,2048]{2,1,0:T(8,128)(2,1)S(1)}, bf16[4,32,2048]{2,1,0:T(8,128)(2,1)S(1)}, u32[]{:S(2)}, u32[]{:S(2)}) %collective-permute-start.1) | collective-permute-done | bytes 524320 | tf_op jit(solution)/shard_map/ppermute | solution.py:99
  33.1 2.9 %collective-permute-done.2.second_ref = bf16[4,32,2048]{2,1,0:T(8,128)(2,1)S(1)} collective-permute-done((bf16[4,32,2048]{2,1,0:T(8,128)(2,1)S(1)}, bf16[4,32,2048]{2,1,0:T(8,128)(2,1)S(1)}, u32[]{:S(2)}, u32[]{:S(2)}) %collective-permute-start.2) | collective-permute-done | bytes 524320 | tf_op jit(solution)/shard_map/ppermute | solution.py:99
  36.0 0.0 copy-done.1
  36.0 1.5 %cluster_sums.1 = bf16[4,32,16,128]{3,2,1,0:T(8,128)(2,1)S(1)} custom-call(s32[1]{0:T(128)} %bitcast.1.replica_ref, s32[32]{0:T(128)S(1)} %copy-done.1, bf16[4,3,2,32,2048]{4,3,2,1,0:T(8,128)(2,1)S(1)} %bitcast.22, bf16[4,3,32,2048]{3,2,1,0:T(8,128)(2,1)S(1)} %collective-permute-done.theirs_ref, bf16[4,32,2048]{2,1,0:T(8,128)(2,1)S(1)} %collective-permute-done.1.first_ref, ...), custom_call_target="tpu_custom_call" | custom-call | tf_op jit(solution)/shard_map/cluster_sums/pallas_call | solution.py:101
  37.6 43.6 %all_to_all.10 = bf16[128,16,128]{2,1,0:T(8,128)(2,1)S(1)} all-to-all(bf16[128,16,128]{2,1,0:T(8,128)(2,1)S(1)} %bitcast.24), channel_id=1, replica_groups={{0,1,2,3,4,5,6,7,8,9,10,11,12,13,14,15,16,17,18,19,20,21,22,23,24,25,26..., dimensions={0} | all-to-all | bytes 1048576 | tf_op jit(solution)/shard_map/all_to_all | solution.py:196
  81.2 0.0 copy-done
  81.2 0.8 momentum.1
  82.0 19.5 %all_gather.3.refs_1_ = bf16[128,2048]{1,0:T(8,128)(2,1)S(1)} all-gather(bf16[32,2048]{1,0:T(8,128)(2,1)S(1)} %get-tuple-element.8), channel_id=1, replica_groups={{0,192,384,576},{32,224,416,608},{64,256,448,640},{96,288,480,672},{128..., dimensions={0}, use_global_device_ids=true | all-gather | bytes 655360 | tf_op jit(solution)/shard_map/all_gather | solution.py:126
  101.5 3.7 %collective-permute-start.3 = (bf16[128,2048]{1,0:T(8,128)(2,1)S(1)}, bf16[128,2048]{1,0:T(8,128)(2,1)S(1)}, u32[]{:S(2)}, u32[]{:S(2)}) collective-permute-start(bf16[128,2048]{1,0:T(8,128)(2,1)S(1)} %all_gather.3.refs_1_), channel_id=1, source_target_pairs={{0,64},{32,736},{64,128},{96,32},{128,192},{160,96},{192,256},{224... | collective-permute-start | bytes 1572872 | tf_op jit(solution)/shard_map/ppermute | solution.py:127
  105.2 3.4 %collective-permute-start.4 = (bf16[128,2048]{1,0:T(8,128)(2,1)S(1)}, bf16[128,2048]{1,0:T(8,128)(2,1)S(1)}, u32[]{:S(2)}, u32[]{:S(2)}) collective-permute-start(bf16[128,2048]{1,0:T(8,128)(2,1)S(1)} %all_gather.3.refs_1_), channel_id=1, source_target_pairs={{0,704},{32,96},{64,0},{96,160},{128,64},{160,224},{192,128},{224,... | collective-permute-start | bytes 1572872 | tf_op jit(solution)/shard_map/ppermute | solution.py:127
  108.5 1.9 %collective-permute-start.5 = (bf16[128,2048]{1,0:T(8,128)(2,1)S(1)}, bf16[128,2048]{1,0:T(8,128)(2,1)S(1)}, u32[]{:S(2)}, u32[]{:S(2)}) collective-permute-start(bf16[128,2048]{1,0:T(8,128)(2,1)S(1)} %all_gather.3.refs_1_), channel_id=1, source_target_pairs={{0,32},{32,0},{64,96},{96,64},{128,160},{160,128},{192,224},{224,1... | collective-permute-start | bytes 1572872 | tf_op jit(solution)/shard_map/ppermute | solution.py:128
  110.5 7.4 %collective-permute-done.3.refs_2_ = bf16[128,2048]{1,0:T(8,128)(2,1)S(1)} collective-permute-done((bf16[128,2048]{1,0:T(8,128)(2,1)S(1)}, bf16[128,2048]{1,0:T(8,128)(2,1)S(1)}, u32[]{:S(2)}, u32[]{:S(2)}) %collective-permute-start.3) | collective-permute-done | bytes 524320 | tf_op jit(solution)/shard_map/ppermute | solution.py:127
  117.8 1.9 %collective-permute-start.6 = (bf16[128,2048]{1,0:T(8,128)(2,1)S(1)}, bf16[128,2048]{1,0:T(8,128)(2,1)S(1)}, u32[]{:S(2)}, u32[]{:S(2)}) collective-permute-start(bf16[128,2048]{1,0:T(8,128)(2,1)S(1)} %collective-permute-done.3.refs_2_), channel_id=1, source_target_pairs={{0,32},{32,0},{64,96},{96,64},{128,160},{160,128},{192,224},{224,1... | collective-permute-start | bytes 1572872 | tf_op jit(solution)/shard_map/ppermute | solution.py:128
  119.8 0.0 collective-permute-done.4.refs_3_
  119.8 2.6 %collective-permute-start.7 = (bf16[128,2048]{1,0:T(8,128)(2,1)S(1)}, bf16[128,2048]{1,0:T(8,128)(2,1)S(1)}, u32[]{:S(2)}, u32[]{:S(2)}) collective-permute-start(bf16[128,2048]{1,0:T(8,128)(2,1)S(1)} %collective-permute-done.4.refs_3_), channel_id=1, source_target_pairs={{0,32},{32,0},{64,96},{96,64},{128,160},{160,128},{192,224},{224,1... | collective-permute-start | bytes 1572872 | tf_op jit(solution)/shard_map/ppermute | solution.py:128
  122.4 0.0 collective-permute-done.5.refs_4_
  122.4 0.0 collective-permute-done.6.refs_5_
  122.4 1.3 collective-permute-done.7.refs_6_
  123.7 6.7 %newton.1 = bf16[32,2048]{1,0:T(8,128)(2,1)S(1)} custom-call(s32[1]{0:T(128)} %bitcast.refs_0_, bf16[128,2048]{1,0:T(8,128)(2,1)S(1)} %all_gather.3.refs_1_, bf16[128,2048]{1,0:T(8,128)(2,1)S(1)} %collective-permute-done.3.refs_2_, bf16[128,2048]{1,0:T(8,128)(2,1)S(1)} %collective-permute-done.4.refs_3_, ...), custom_call_target="tpu_custom_call" | custom-call | tf_op jit(solution)/shard_map/newton/pallas_call | solution.py:174
  130.4 16.8 %all_to_all.11 = bf16[32,16,128]{2,1,0:T(8,128)(2,1)S(1)} all-to-all(bf16[32,16,128]{2,1,0:T(8,128)(2,1)S(1)} %bitcast.28), channel_id=1, replica_groups=mesh['rep'=24,'fsdp'=32] {'fsdp'}, dimensions={0} | all-to-all | bytes 262144 | tf_op jit(solution)/shard_map/all_to_all | solution.py:204
  147.2 0.9 fusion
  (1 shorter events, 0.0 us)
Async XLA Ops:
  4.4 31.6 %copy-start.1 = (s32[32]{0:T(128)S(1)}, s32[32]{0:T(128)}, u32[]{:S(2)}) copy-start(s32[32]{0:T(128)} %owner_ref.1) | copy-start | bytes 388
  4.4 5.3 %collective-permute-start = (bf16[4,3,32,2048]{3,2,1,0:T(8,128)(2,1)S(1)}, bf16[4,3,32,2048]{3,2,1,0:T(8,128)(2,1)S(1)}, u32[]{:S(2)}, u32[]{:S(2)}) collective-permute-start(bf16[4,3,32,2048]{3,2,1,0:T(8,128)(2,1)S(1)} %dynamic-slice_bitcast_fusion), channel_id=1, source_target_pairs={{0,32},{32,0},{64,96},{96,64},{128,160},{160,128},{192,224},{224,1... | collective-permute-start | bytes 4718600 | tf_op jit(solution)/shard_map/ppermute | solution.py:89
  9.9 23.2 %collective-permute-start.1 = (bf16[4,32,2048]{2,1,0:T(8,128)(2,1)S(1)}, bf16[4,32,2048]{2,1,0:T(8,128)(2,1)S(1)}, u32[]{:S(2)}, u32[]{:S(2)}) collective-permute-start(bf16[4,32,2048]{2,1,0:T(8,128)(2,1)S(1)} %get-tuple-element.6), channel_id=1, source_target_pairs={{0,64},{32,736},{64,128},{96,32},{128,192},{160,96},{192,256},{224... | collective-permute-start | bytes 1572872 | tf_op jit(solution)/shard_map/ppermute | solution.py:99
  14.2 66.9 %copy-start = (f32[1,32,1,2048]{3,2,1,0:T(1,128)S(1)}, f32[1,32,1,2048]{3,2,1,0:T(1,128)}, u32[]{:S(2)}) copy-start(f32[1,32,1,2048]{3,2,1,0:T(1,128)} %param.4) | copy-start | bytes 786436
  14.2 21.8 %collective-permute-start.2 = (bf16[4,32,2048]{2,1,0:T(8,128)(2,1)S(1)}, bf16[4,32,2048]{2,1,0:T(8,128)(2,1)S(1)}, u32[]{:S(2)}, u32[]{:S(2)}) collective-permute-start(bf16[4,32,2048]{2,1,0:T(8,128)(2,1)S(1)} %get-tuple-element.7), channel_id=1, source_target_pairs={{0,704},{32,96},{64,0},{96,160},{128,64},{160,224},{192,128},{224,... | collective-permute-start | bytes 1572872 | tf_op jit(solution)/shard_map/ppermute | solution.py:99
  101.5 16.4 %collective-permute-start.3 = (bf16[128,2048]{1,0:T(8,128)(2,1)S(1)}, bf16[128,2048]{1,0:T(8,128)(2,1)S(1)}, u32[]{:S(2)}, u32[]{:S(2)}) collective-permute-start(bf16[128,2048]{1,0:T(8,128)(2,1)S(1)} %all_gather.3.refs_1_), channel_id=1, source_target_pairs={{0,64},{32,736},{64,128},{96,32},{128,192},{160,96},{192,256},{224... | collective-permute-start | bytes 1572872 | tf_op jit(solution)/shard_map/ppermute | solution.py:127
  105.2 14.6 %collective-permute-start.4 = (bf16[128,2048]{1,0:T(8,128)(2,1)S(1)}, bf16[128,2048]{1,0:T(8,128)(2,1)S(1)}, u32[]{:S(2)}, u32[]{:S(2)}) collective-permute-start(bf16[128,2048]{1,0:T(8,128)(2,1)S(1)} %all_gather.3.refs_1_), channel_id=1, source_target_pairs={{0,704},{32,96},{64,0},{96,160},{128,64},{160,224},{192,128},{224,... | collective-permute-start | bytes 1572872 | tf_op jit(solution)/shard_map/ppermute | solution.py:127
  108.5 13.9 %collective-permute-start.5 = (bf16[128,2048]{1,0:T(8,128)(2,1)S(1)}, bf16[128,2048]{1,0:T(8,128)(2,1)S(1)}, u32[]{:S(2)}, u32[]{:S(2)}) collective-permute-start(bf16[128,2048]{1,0:T(8,128)(2,1)S(1)} %all_gather.3.refs_1_), channel_id=1, source_target_pairs={{0,32},{32,0},{64,96},{96,64},{128,160},{160,128},{192,224},{224,1... | collective-permute-start | bytes 1572872 | tf_op jit(solution)/shard_map/ppermute | solution.py:128
  117.8 4.6 %collective-permute-start.6 = (bf16[128,2048]{1,0:T(8,128)(2,1)S(1)}, bf16[128,2048]{1,0:T(8,128)(2,1)S(1)}, u32[]{:S(2)}, u32[]{:S(2)}) collective-permute-start(bf16[128,2048]{1,0:T(8,128)(2,1)S(1)} %collective-permute-done.3.refs_2_), channel_id=1, source_target_pairs={{0,32},{32,0},{64,96},{96,64},{128,160},{160,128},{192,224},{224,1... | collective-permute-start | bytes 1572872 | tf_op jit(solution)/shard_map/ppermute | solution.py:128
  119.8 3.9 %collective-permute-start.7 = (bf16[128,2048]{1,0:T(8,128)(2,1)S(1)}, bf16[128,2048]{1,0:T(8,128)(2,1)S(1)}, u32[]{:S(2)}, u32[]{:S(2)}) collective-permute-start(bf16[128,2048]{1,0:T(8,128)(2,1)S(1)} %collective-permute-done.4.refs_3_), channel_id=1, source_target_pairs={{0,32},{32,0},{64,96},{96,64},{128,160},{160,128},{192,224},{224,1... | collective-permute-start | bytes 1572872 | tf_op jit(solution)/shard_map/ppermute | solution.py:128

commit v5 on v4

--- a/solution.py
+++ b/solution.py
@@ -124,7 +124,8 @@
 
 def gather_rows(rows, replicas):
     own = lax.all_gather(rows, "rep", axis=0, tiled=True, axis_index_groups=classes(replicas))
-    pieces = [own] + [lax.ppermute(own, "rep", neighbours(turn, replicas)) for turn in range(2)]
+    near = [lax.ppermute(own, "rep", neighbours(turn, replicas)) for turn in range(2)]
+    pieces = [own, *lax.optimization_barrier(near)]
     return pieces + [lax.ppermute(piece, "rep", other_core(replicas)) for piece in pieces]
 
 

time: 149 us -> 149 us (level)
  no operation moved by 1% of the time
where the time goes in v5:
time: 149 us; the launch traced here: 148 us
  blocking collectives  78.9 us (53%)
  starting transfers between devices  32.9 us (22%)
  waiting for transfers between devices  21.8 us (15%)
  Pallas kernels  9.26 us (6%)
  local copies, waits for them, and re-layouts  3.76 us (3%)
    all_to_all x1, blocking collectives, on_device(): lax.all_to_all(sums.reshape(members * slots, *tiled[1:]), ('rep', 'fsdp')...  43.6 us
    all_gather x1, blocking collectives, gather_rows(): lax.all_gather(rows, 'rep', axis=0, tiled=True, axis_index_groups=classes...  19.5 us
    ppermute x2, starting transfers between devices, cluster_sums(): lax.ppermute(sums, 'rep', neighbours(turn, replicas))  16.6 us
    all_to_all x1, blocking collectives, on_device(): lax.all_to_all(update_rows.reshape(tiled), 'fsdp', split_axis=0, concat_a...  15.8 us
    ppermute x2, waiting for transfers between devices, cluster_sums(): lax.ppermute(sums, 'rep', neighbours(turn, replicas))  9.39 us
    ppermute x2, waiting for transfers between devices, gather_rows(): lax.ppermute(own, 'rep', neighbours(turn, replicas))  7.38 us
    ppermute x3, starting transfers between devices, gather_rows(): lax.ppermute(piece, 'rep', other_core(replicas))  7.27 us
    ppermute x2, starting transfers between devices, gather_rows(): lax.ppermute(own, 'rep', neighbours(turn, replicas))  7.04 us
  transfers between devices with their start and end apart: 8, of which 5 were waited for; matrix products, arithmetic and copies ran while one was open for 0% of the time, Pallas kernels for 0%

profile of v5, /device:TPU:8, one launch (start us, length us, event | category | flops | bytes accessed | tf_op | source)
XLA Modules:
  0.0 148.3 jit_solution(13188814682914566485)
XLA Ops:
  0.6 3.6 %copy.5 = bf16[24,32,2048]{2,1,0:T(8,128)(2,1)S(1)} copy(bf16[24,32,2048]{2,0,1:T(8,128)(2,1)} %bitcast.27) | data formatting | bytes 6291456 | tf_op jit(solution)/shard_map/transpose | solution.py:88
  4.3 0.1 dynamic-slice_bitcast_fusion
  4.4 0.0 copy-start.1
  4.4 1.9 %collective-permute-start = (bf16[4,3,32,2048]{3,2,1,0:T(8,128)(2,1)S(1)}, bf16[4,3,32,2048]{3,2,1,0:T(8,128)(2,1)S(1)}, u32[]{:S(2)}, u32[]{:S(2)}) collective-permute-start(bf16[4,3,32,2048]{3,2,1,0:T(8,128)(2,1)S(1)} %dynamic-slice_bitcast_fusion), channel_id=1, source_target_pairs={{0,32},{32,0},{64,96},{96,64},{128,160},{160,128},{192,224},{224,1... | collective-permute-start | bytes 4718600 | tf_op jit(solution)/shard_map/ppermute | solution.py:89
  6.3 3.4 %collective-permute-done.theirs_ref = bf16[4,3,32,2048]{3,2,1,0:T(8,128)(2,1)S(1)} collective-permute-done((bf16[4,3,32,2048]{3,2,1,0:T(8,128)(2,1)S(1)}, bf16[4,3,32,2048]{3,2,1,0:T(8,128)(2,1)S(1)}, u32[]{:S(2)}, u32[]{:S(2)}) %collective-permute-start) | collective-permute-done | bytes 1572896 | tf_op jit(solution)/shard_map/ppermute | solution.py:89
  9.7 0.2 chip_sums.1
  9.9 4.3 %collective-permute-start.1 = (bf16[4,32,2048]{2,1,0:T(8,128)(2,1)S(1)}, bf16[4,32,2048]{2,1,0:T(8,128)(2,1)S(1)}, u32[]{:S(2)}, u32[]{:S(2)}) collective-permute-start(bf16[4,32,2048]{2,1,0:T(8,128)(2,1)S(1)} %get-tuple-element.8), channel_id=1, source_target_pairs={{0,64},{32,736},{64,128},{96,32},{128,192},{160,96},{192,256},{224... | collective-permute-start | bytes 1572872 | tf_op jit(solution)/shard_map/ppermute | solution.py:99
  14.2 0.0 copy-start
  14.2 12.4 %collective-permute-start.2 = (bf16[4,32,2048]{2,1,0:T(8,128)(2,1)S(1)}, bf16[4,32,2048]{2,1,0:T(8,128)(2,1)S(1)}, u32[]{:S(2)}, u32[]{:S(2)}) collective-permute-start(bf16[4,32,2048]{2,1,0:T(8,128)(2,1)S(1)} %get-tuple-element.9), channel_id=1, source_target_pairs={{0,704},{32,96},{64,0},{96,160},{128,64},{160,224},{192,128},{224,... | collective-permute-start | bytes 1572872 | tf_op jit(solution)/shard_map/ppermute | solution.py:99
  26.6 6.5 %collective-permute-done.1.first_ref = bf16[4,32,2048]{2,1,0:T(8,128)(2,1)S(1)} collective-permute-done((bf16[4,32,2048]{2,1,0:T(8,128)(2,1)S(1)}, bf16[4,32,2048]{2,1,0:T(8,128)(2,1)S(1)}, u32[]{:S(2)}, u32[]{:S(2)}) %collective-permute-start.1) | collective-permute-done | bytes 524320 | tf_op jit(solution)/shard_map/ppermute | solution.py:99
  33.1 2.9 %collective-permute-done.2.second_ref = bf16[4,32,2048]{2,1,0:T(8,128)(2,1)S(1)} collective-permute-done((bf16[4,32,2048]{2,1,0:T(8,128)(2,1)S(1)}, bf16[4,32,2048]{2,1,0:T(8,128)(2,1)S(1)}, u32[]{:S(2)}, u32[]{:S(2)}) %collective-permute-start.2) | collective-permute-done | bytes 524320 | tf_op jit(solution)/shard_map/ppermute | solution.py:99
  36.0 0.0 copy-done.1
  36.0 1.5 %cluster_sums.1 = bf16[4,32,16,128]{3,2,1,0:T(8,128)(2,1)S(1)} custom-call(s32[1]{0:T(128)} %bitcast.1.replica_ref, s32[32]{0:T(128)S(1)} %copy-done.1, bf16[4,3,2,32,2048]{4,3,2,1,0:T(8,128)(2,1)S(1)} %bitcast.22, bf16[4,3,32,2048]{3,2,1,0:T(8,128)(2,1)S(1)} %collective-permute-done.theirs_ref, bf16[4,32,2048]{2,1,0:T(8,128)(2,1)S(1)} %collective-permute-done.1.first_ref, ...), custom_call_target="tpu_custom_call" | custom-call | tf_op jit(solution)/shard_map/cluster_sums/pallas_call | solution.py:101
  37.6 43.6 %all_to_all.10 = bf16[128,16,128]{2,1,0:T(8,128)(2,1)S(1)} all-to-all(bf16[128,16,128]{2,1,0:T(8,128)(2,1)S(1)} %bitcast.24), channel_id=1, replica_groups={{0,1,2,3,4,5,6,7,8,9,10,11,12,13,14,15,16,17,18,19,20,21,22,23,24,25,26..., dimensions={0} | all-to-all | bytes 1048576 | tf_op jit(solution)/shard_map/all_to_all | solution.py:197
  81.2 0.0 copy-done
  81.2 0.8 momentum.1
  82.0 19.5 %all_gather.3.refs_1_ = bf16[128,2048]{1,0:T(8,128)(2,1)S(1)} all-gather(bf16[32,2048]{1,0:T(8,128)(2,1)S(1)} %get-tuple-element.10), channel_id=1, replica_groups={{0,192,384,576},{32,224,416,608},{64,256,448,640},{96,288,480,672},{128..., dimensions={0}, use_global_device_ids=true | all-gather | bytes 655360 | tf_op jit(solution)/shard_map/all_gather | solution.py:126
  101.5 3.7 %collective-permute-start.3 = (bf16[128,2048]{1,0:T(8,128)(2,1)S(1)}, bf16[128,2048]{1,0:T(8,128)(2,1)S(1)}, u32[]{:S(2)}, u32[]{:S(2)}) collective-permute-start(bf16[128,2048]{1,0:T(8,128)(2,1)S(1)} %all_gather.3.refs_1_), channel_id=1, source_target_pairs={{0,64},{32,736},{64,128},{96,32},{128,192},{160,96},{192,256},{224... | collective-permute-start | bytes 1572872 | tf_op jit(solution)/shard_map/ppermute | solution.py:127
  105.2 3.4 %collective-permute-start.4 = (bf16[128,2048]{1,0:T(8,128)(2,1)S(1)}, bf16[128,2048]{1,0:T(8,128)(2,1)S(1)}, u32[]{:S(2)}, u32[]{:S(2)}) collective-permute-start(bf16[128,2048]{1,0:T(8,128)(2,1)S(1)} %all_gather.3.refs_1_), channel_id=1, source_target_pairs={{0,704},{32,96},{64,0},{96,160},{128,64},{160,224},{192,128},{224,... | collective-permute-start | bytes 1572872 | tf_op jit(solution)/shard_map/ppermute | solution.py:127
  108.5 1.9 %collective-permute-start.5 = (bf16[128,2048]{1,0:T(8,128)(2,1)S(1)}, bf16[128,2048]{1,0:T(8,128)(2,1)S(1)}, u32[]{:S(2)}, u32[]{:S(2)}) collective-permute-start(bf16[128,2048]{1,0:T(8,128)(2,1)S(1)} %all_gather.3.refs_1_), channel_id=1, source_target_pairs={{0,32},{32,0},{64,96},{96,64},{128,160},{160,128},{192,224},{224,1... | collective-permute-start | bytes 1572872 | tf_op jit(solution)/shard_map/ppermute | solution.py:129
  110.5 7.4 %collective-permute-done.3.refs_2_ = bf16[128,2048]{1,0:T(8,128)(2,1)S(1)} collective-permute-done((bf16[128,2048]{1,0:T(8,128)(2,1)S(1)}, bf16[128,2048]{1,0:T(8,128)(2,1)S(1)}, u32[]{:S(2)}, u32[]{:S(2)}) %collective-permute-start.3) | collective-permute-done | bytes 524320 | tf_op jit(solution)/shard_map/ppermute | solution.py:127
  117.8 0.0 collective-permute-done.4.refs_3_
  117.8 3.2 %collective-permute-start.6 = (bf16[128,2048]{1,0:T(8,128)(2,1)S(1)}, bf16[128,2048]{1,0:T(8,128)(2,1)S(1)}, u32[]{:S(2)}, u32[]{:S(2)}) collective-permute-start(bf16[128,2048]{1,0:T(8,128)(2,1)S(1)} %collective-permute-done.3.refs_2_), channel_id=1, source_target_pairs={{0,32},{32,0},{64,96},{96,64},{128,160},{160,128},{192,224},{224,1... | collective-permute-start | bytes 1572872 | tf_op jit(solution)/shard_map/ppermute | solution.py:129
  121.1 2.1 %collective-permute-start.7 = (bf16[128,2048]{1,0:T(8,128)(2,1)S(1)}, bf16[128,2048]{1,0:T(8,128)(2,1)S(1)}, u32[]{:S(2)}, u32[]{:S(2)}) collective-permute-start(bf16[128,2048]{1,0:T(8,128)(2,1)S(1)} %collective-permute-done.4.refs_3_), channel_id=1, source_target_pairs={{0,32},{32,0},{64,96},{96,64},{128,160},{160,128},{192,224},{224,1... | collective-permute-start | bytes 1572872 | tf_op jit(solution)/shard_map/ppermute | solution.py:129
  123.2 0.0 collective-permute-done.5.refs_4_
  123.2 0.0 collective-permute-done.6.refs_5_
  123.3 1.7 %collective-permute-done.7.refs_6_ = bf16[128,2048]{1,0:T(8,128)(2,1)S(1)} collective-permute-done((bf16[128,2048]{1,0:T(8,128)(2,1)S(1)}, bf16[128,2048]{1,0:T(8,128)(2,1)S(1)}, u32[]{:S(2)}, u32[]{:S(2)}) %collective-permute-start.7) | collective-permute-done | bytes 524320 | tf_op jit(solution)/shard_map/ppermute | solution.py:129
  124.9 6.7 %newton.1 = bf16[32,2048]{1,0:T(8,128)(2,1)S(1)} custom-call(s32[1]{0:T(128)} %bitcast.refs_0_, bf16[128,2048]{1,0:T(8,128)(2,1)S(1)} %all_gather.3.refs_1_, bf16[128,2048]{1,0:T(8,128)(2,1)S(1)} %collective-permute-done.3.refs_2_, bf16[128,2048]{1,0:T(8,128)(2,1)S(1)} %collective-permute-done.4.refs_3_, ...), custom_call_target="tpu_custom_call" | custom-call | tf_op jit(solution)/shard_map/newton/pallas_call | solution.py:175
  131.6 15.8 %all_to_all.11 = bf16[32,16,128]{2,1,0:T(8,128)(2,1)S(1)} all-to-all(bf16[32,16,128]{2,1,0:T(8,128)(2,1)S(1)} %bitcast.28), channel_id=1, replica_groups=mesh['rep'=24,'fsdp'=32] {'fsdp'}, dimensions={0} | all-to-all | bytes 262144 | tf_op jit(solution)/shard_map/all_to_all | solution.py:205
  147.4 0.9 fusion
  (1 shorter events, 0.0 us)
Async XLA Ops:
  4.4 31.6 %copy-start.1 = (s32[32]{0:T(128)S(1)}, s32[32]{0:T(128)}, u32[]{:S(2)}) copy-start(s32[32]{0:T(128)} %owner_ref.1) | copy-start | bytes 388
  4.4 5.3 %collective-permute-start = (bf16[4,3,32,2048]{3,2,1,0:T(8,128)(2,1)S(1)}, bf16[4,3,32,2048]{3,2,1,0:T(8,128)(2,1)S(1)}, u32[]{:S(2)}, u32[]{:S(2)}) collective-permute-start(bf16[4,3,32,2048]{3,2,1,0:T(8,128)(2,1)S(1)} %dynamic-slice_bitcast_fusion), channel_id=1, source_target_pairs={{0,32},{32,0},{64,96},{96,64},{128,160},{160,128},{192,224},{224,1... | collective-permute-start | bytes 4718600 | tf_op jit(solution)/shard_map/ppermute | solution.py:89
  9.9 23.2 %collective-permute-start.1 = (bf16[4,32,2048]{2,1,0:T(8,128)(2,1)S(1)}, bf16[4,32,2048]{2,1,0:T(8,128)(2,1)S(1)}, u32[]{:S(2)}, u32[]{:S(2)}) collective-permute-start(bf16[4,32,2048]{2,1,0:T(8,128)(2,1)S(1)} %get-tuple-element.8), channel_id=1, source_target_pairs={{0,64},{32,736},{64,128},{96,32},{128,192},{160,96},{192,256},{224... | collective-permute-start | bytes 1572872 | tf_op jit(solution)/shard_map/ppermute | solution.py:99
  14.2 66.9 %copy-start = (f32[1,32,1,2048]{3,2,1,0:T(1,128)S(1)}, f32[1,32,1,2048]{3,2,1,0:T(1,128)}, u32[]{:S(2)}) copy-start(f32[1,32,1,2048]{3,2,1,0:T(1,128)} %param.4) | copy-start | bytes 786436
  14.2 21.8 %collective-permute-start.2 = (bf16[4,32,2048]{2,1,0:T(8,128)(2,1)S(1)}, bf16[4,32,2048]{2,1,0:T(8,128)(2,1)S(1)}, u32[]{:S(2)}, u32[]{:S(2)}) collective-permute-start(bf16[4,32,2048]{2,1,0:T(8,128)(2,1)S(1)} %get-tuple-element.9), channel_id=1, source_target_pairs={{0,704},{32,96},{64,0},{96,160},{128,64},{160,224},{192,128},{224,... | collective-permute-start | bytes 1572872 | tf_op jit(solution)/shard_map/ppermute | solution.py:99
  101.5 16.4 %collective-permute-start.3 = (bf16[128,2048]{1,0:T(8,128)(2,1)S(1)}, bf16[128,2048]{1,0:T(8,128)(2,1)S(1)}, u32[]{:S(2)}, u32[]{:S(2)}) collective-permute-start(bf16[128,2048]{1,0:T(8,128)(2,1)S(1)} %all_gather.3.refs_1_), channel_id=1, source_target_pairs={{0,64},{32,736},{64,128},{96,32},{128,192},{160,96},{192,256},{224... | collective-permute-start | bytes 1572872 | tf_op jit(solution)/shard_map/ppermute | solution.py:127
  105.2 12.7 %collective-permute-start.4 = (bf16[128,2048]{1,0:T(8,128)(2,1)S(1)}, bf16[128,2048]{1,0:T(8,128)(2,1)S(1)}, u32[]{:S(2)}, u32[]{:S(2)}) collective-permute-start(bf16[128,2048]{1,0:T(8,128)(2,1)S(1)} %all_gather.3.refs_1_), channel_id=1, source_target_pairs={{0,704},{32,96},{64,0},{96,160},{128,64},{160,224},{192,128},{224,... | collective-permute-start | bytes 1572872 | tf_op jit(solution)/shard_map/ppermute | solution.py:127
  108.5 14.7 %collective-permute-start.5 = (bf16[128,2048]{1,0:T(8,128)(2,1)S(1)}, bf16[128,2048]{1,0:T(8,128)(2,1)S(1)}, u32[]{:S(2)}, u32[]{:S(2)}) collective-permute-start(bf16[128,2048]{1,0:T(8,128)(2,1)S(1)} %all_gather.3.refs_1_), channel_id=1, source_target_pairs={{0,32},{32,0},{64,96},{96,64},{128,160},{160,128},{192,224},{224,1... | collective-permute-start | bytes 1572872 | tf_op jit(solution)/shard_map/ppermute | solution.py:129
  117.8 5.4 %collective-permute-start.6 = (bf16[128,2048]{1,0:T(8,128)(2,1)S(1)}, bf16[128,2048]{1,0:T(8,128)(2,1)S(1)}, u32[]{:S(2)}, u32[]{:S(2)}) collective-permute-start(bf16[128,2048]{1,0:T(8,128)(2,1)S(1)} %collective-permute-done.3.refs_2_), channel_id=1, source_target_pairs={{0,32},{32,0},{64,96},{96,64},{128,160},{160,128},{192,224},{224,1... | collective-permute-start | bytes 1572872 | tf_op jit(solution)/shard_map/ppermute | solution.py:129
  121.1 3.8 %collective-permute-start.7 = (bf16[128,2048]{1,0:T(8,128)(2,1)S(1)}, bf16[128,2048]{1,0:T(8,128)(2,1)S(1)}, u32[]{:S(2)}, u32[]{:S(2)}) collective-permute-start(bf16[128,2048]{1,0:T(8,128)(2,1)S(1)} %collective-permute-done.4.refs_3_), channel_id=1, source_target_pairs={{0,32},{32,0},{64,96},{96,64},{128,160},{160,128},{192,224},{224,1... | collective-permute-start | bytes 1572872 | tf_op jit(solution)/shard_map/ppermute | solution.py:129

commit v6 on v4

--- a/solution.py
+++ b/solution.py
@@ -124,7 +124,8 @@
 
 def gather_rows(rows, replicas):
     own = lax.all_gather(rows, "rep", axis=0, tiled=True, axis_index_groups=classes(replicas))
-    pieces = [own] + [lax.ppermute(own, "rep", neighbours(turn, replicas)) for turn in range(2)]
+    ways = [[(r, (r + way) % replicas) for r in range(replicas)] for way in (2, -2)]
+    pieces = [own] + [lax.ppermute(own, "rep", way) for way in ways]
     return pieces + [lax.ppermute(piece, "rep", other_core(replicas)) for piece in pieces]
 
 

time: 149 us -> 148 us (level)
  waiting for transfers between devices: 21.4 us -> 19.9 us
    ppermute x2, waiting for transfers between devices: 7.38 us -> 5.85 us  [gather_rows(): pieces = [own] + [lax.ppermute(own, 'rep', way) for way in ways]]
where the time goes in v6:
time: 148 us; the launch traced here: 147 us
  blocking collectives  80.6 us (54%)
  starting transfers between devices  32 us (22%)
  waiting for transfers between devices  19.9 us (13%)
  Pallas kernels  9.26 us (6%)
  local copies, waits for them, and re-layouts  3.76 us (3%)
    all_to_all x1, blocking collectives, on_device(): lax.all_to_all(sums.reshape(members * slots, *tiled[1:]), ('rep', 'fsdp')...  43.6 us
    all_gather x1, blocking collectives, gather_rows(): lax.all_gather(rows, 'rep', axis=0, tiled=True, axis_index_groups=classes...  19.5 us
    all_to_all x1, blocking collectives, on_device(): lax.all_to_all(update_rows.reshape(tiled), 'fsdp', split_axis=0, concat_a...  17.5 us
    ppermute x2, starting transfers between devices, cluster_sums(): lax.ppermute(sums, 'rep', neighbours(turn, replicas))  16.6 us
    ppermute x2, waiting for transfers between devices, cluster_sums(): lax.ppermute(sums, 'rep', neighbours(turn, replicas))  9.39 us
    ppermute x2, starting transfers between devices, gather_rows(): pieces = [own] + [lax.ppermute(own, 'rep', way) for way in ways]  7.04 us
    pallas_call x1, Pallas kernels, newton_rows(): pl.pallas_call(lambda *refs: newton_kernel(count, factor, *refs), out_sha...  6.66 us
    ppermute x3, starting transfers between devices, gather_rows(): lax.ppermute(piece, 'rep', other_core(replicas))  6.42 us
  transfers between devices with their start and end apart: 8, of which 5 were waited for; matrix products, arithmetic and copies ran while one was open for 0% of the time, Pallas kernels for 0%

profile of v6, /device:TPU:8, one launch (start us, length us, event | category | flops | bytes accessed | tf_op | source)
XLA Modules:
  0.0 147.3 jit_solution(1074174971598338125)
XLA Ops:
  0.6 3.6 %copy.5 = bf16[24,32,2048]{2,1,0:T(8,128)(2,1)S(1)} copy(bf16[24,32,2048]{2,0,1:T(8,128)(2,1)} %bitcast.27) | data formatting | bytes 6291456 | tf_op jit(solution)/shard_map/transpose | solution.py:88
  4.3 0.1 dynamic-slice_bitcast_fusion
  4.4 0.0 copy-start.1
  4.4 1.9 %collective-permute-start = (bf16[4,3,32,2048]{3,2,1,0:T(8,128)(2,1)S(1)}, bf16[4,3,32,2048]{3,2,1,0:T(8,128)(2,1)S(1)}, u32[]{:S(2)}, u32[]{:S(2)}) collective-permute-start(bf16[4,3,32,2048]{3,2,1,0:T(8,128)(2,1)S(1)} %dynamic-slice_bitcast_fusion), channel_id=1, source_target_pairs={{0,32},{32,0},{64,96},{96,64},{128,160},{160,128},{192,224},{224,1... | collective-permute-start | bytes 4718600 | tf_op jit(solution)/shard_map/ppermute | solution.py:89
  6.3 3.4 %collective-permute-done.theirs_ref = bf16[4,3,32,2048]{3,2,1,0:T(8,128)(2,1)S(1)} collective-permute-done((bf16[4,3,32,2048]{3,2,1,0:T(8,128)(2,1)S(1)}, bf16[4,3,32,2048]{3,2,1,0:T(8,128)(2,1)S(1)}, u32[]{:S(2)}, u32[]{:S(2)}) %collective-permute-start) | collective-permute-done | bytes 1572896 | tf_op jit(solution)/shard_map/ppermute | solution.py:89
  9.7 0.2 chip_sums.1
  9.9 4.3 %collective-permute-start.1 = (bf16[4,32,2048]{2,1,0:T(8,128)(2,1)S(1)}, bf16[4,32,2048]{2,1,0:T(8,128)(2,1)S(1)}, u32[]{:S(2)}, u32[]{:S(2)}) collective-permute-start(bf16[4,32,2048]{2,1,0:T(8,128)(2,1)S(1)} %get-tuple-element.6), channel_id=1, source_target_pairs={{0,64},{32,736},{64,128},{96,32},{128,192},{160,96},{192,256},{224... | collective-permute-start | bytes 1572872 | tf_op jit(solution)/shard_map/ppermute | solution.py:99
  14.2 0.0 copy-start
  14.2 12.4 %collective-permute-start.2 = (bf16[4,32,2048]{2,1,0:T(8,128)(2,1)S(1)}, bf16[4,32,2048]{2,1,0:T(8,128)(2,1)S(1)}, u32[]{:S(2)}, u32[]{:S(2)}) collective-permute-start(bf16[4,32,2048]{2,1,0:T(8,128)(2,1)S(1)} %get-tuple-element.7), channel_id=1, source_target_pairs={{0,704},{32,96},{64,0},{96,160},{128,64},{160,224},{192,128},{224,... | collective-permute-start | bytes 1572872 | tf_op jit(solution)/shard_map/ppermute | solution.py:99
  26.6 6.5 %collective-permute-done.1.first_ref = bf16[4,32,2048]{2,1,0:T(8,128)(2,1)S(1)} collective-permute-done((bf16[4,32,2048]{2,1,0:T(8,128)(2,1)S(1)}, bf16[4,32,2048]{2,1,0:T(8,128)(2,1)S(1)}, u32[]{:S(2)}, u32[]{:S(2)}) %collective-permute-start.1) | collective-permute-done | bytes 524320 | tf_op jit(solution)/shard_map/ppermute | solution.py:99
  33.1 2.9 %collective-permute-done.2.second_ref = bf16[4,32,2048]{2,1,0:T(8,128)(2,1)S(1)} collective-permute-done((bf16[4,32,2048]{2,1,0:T(8,128)(2,1)S(1)}, bf16[4,32,2048]{2,1,0:T(8,128)(2,1)S(1)}, u32[]{:S(2)}, u32[]{:S(2)}) %collective-permute-start.2) | collective-permute-done | bytes 524320 | tf_op jit(solution)/shard_map/ppermute | solution.py:99
  36.0 0.0 copy-done.1
  36.0 1.5 %cluster_sums.1 = bf16[4,32,16,128]{3,2,1,0:T(8,128)(2,1)S(1)} custom-call(s32[1]{0:T(128)} %bitcast.1.replica_ref, s32[32]{0:T(128)S(1)} %copy-done.1, bf16[4,3,2,32,2048]{4,3,2,1,0:T(8,128)(2,1)S(1)} %bitcast.22, bf16[4,3,32,2048]{3,2,1,0:T(8,128)(2,1)S(1)} %collective-permute-done.theirs_ref, bf16[4,32,2048]{2,1,0:T(8,128)(2,1)S(1)} %collective-permute-done.1.first_ref, ...), custom_call_target="tpu_custom_call" | custom-call | tf_op jit(solution)/shard_map/cluster_sums/pallas_call | solution.py:101
  37.6 43.6 %all_to_all.10 = bf16[128,16,128]{2,1,0:T(8,128)(2,1)S(1)} all-to-all(bf16[128,16,128]{2,1,0:T(8,128)(2,1)S(1)} %bitcast.24), channel_id=1, replica_groups={{0,1,2,3,4,5,6,7,8,9,10,11,12,13,14,15,16,17,18,19,20,21,22,23,24,25,26..., dimensions={0} | all-to-all | bytes 1048576 | tf_op jit(solution)/shard_map/all_to_all | solution.py:197
  81.2 0.0 copy-done
  81.2 0.8 momentum.1
  82.0 19.5 %all_gather.3.refs_1_ = bf16[128,2048]{1,0:T(8,128)(2,1)S(1)} all-gather(bf16[32,2048]{1,0:T(8,128)(2,1)S(1)} %get-tuple-element.8), channel_id=1, replica_groups={{0,192,384,576},{32,224,416,608},{64,256,448,640},{96,288,480,672},{128..., dimensions={0}, use_global_device_ids=true | all-gather | bytes 655360 | tf_op jit(solution)/shard_map/all_gather | solution.py:126
  101.5 3.8 %collective-permute-start.3 = (bf16[128,2048]{1,0:T(8,128)(2,1)S(1)}, bf16[128,2048]{1,0:T(8,128)(2,1)S(1)}, u32[]{:S(2)}, u32[]{:S(2)}) collective-permute-start(bf16[128,2048]{1,0:T(8,128)(2,1)S(1)} %all_gather.3.refs_1_), channel_id=1, source_target_pairs={{0,64},{32,96},{64,128},{96,160},{128,192},{160,224},{192,256},{22... | collective-permute-start | bytes 1572872 | tf_op jit(solution)/shard_map/ppermute | solution.py:128
  105.3 3.3 %collective-permute-start.4 = (bf16[128,2048]{1,0:T(8,128)(2,1)S(1)}, bf16[128,2048]{1,0:T(8,128)(2,1)S(1)}, u32[]{:S(2)}, u32[]{:S(2)}) collective-permute-start(bf16[128,2048]{1,0:T(8,128)(2,1)S(1)} %all_gather.3.refs_1_), channel_id=1, source_target_pairs={{0,704},{32,736},{64,0},{96,32},{128,64},{160,96},{192,128},{224,1... | collective-permute-start | bytes 1572872 | tf_op jit(solution)/shard_map/ppermute | solution.py:128
  108.5 1.9 %collective-permute-start.5 = (bf16[128,2048]{1,0:T(8,128)(2,1)S(1)}, bf16[128,2048]{1,0:T(8,128)(2,1)S(1)}, u32[]{:S(2)}, u32[]{:S(2)}) collective-permute-start(bf16[128,2048]{1,0:T(8,128)(2,1)S(1)} %all_gather.3.refs_1_), channel_id=1, source_target_pairs={{0,32},{32,0},{64,96},{96,64},{128,160},{160,128},{192,224},{224,1... | collective-permute-start | bytes 1572872 | tf_op jit(solution)/shard_map/ppermute | solution.py:129
  110.5 5.9 %collective-permute-done.3.refs_2_ = bf16[128,2048]{1,0:T(8,128)(2,1)S(1)} collective-permute-done((bf16[128,2048]{1,0:T(8,128)(2,1)S(1)}, bf16[128,2048]{1,0:T(8,128)(2,1)S(1)}, u32[]{:S(2)}, u32[]{:S(2)}) %collective-permute-start.3) | collective-permute-done | bytes 524320 | tf_op jit(solution)/shard_map/ppermute | solution.py:128
  116.3 1.9 %collective-permute-start.6 = (bf16[128,2048]{1,0:T(8,128)(2,1)S(1)}, bf16[128,2048]{1,0:T(8,128)(2,1)S(1)}, u32[]{:S(2)}, u32[]{:S(2)}) collective-permute-start(bf16[128,2048]{1,0:T(8,128)(2,1)S(1)} %collective-permute-done.3.refs_2_), channel_id=1, source_target_pairs={{0,32},{32,0},{64,96},{96,64},{128,160},{160,128},{192,224},{224,1... | collective-permute-start | bytes 1572872 | tf_op jit(solution)/shard_map/ppermute | solution.py:129
  118.2 0.0 collective-permute-done.4.refs_3_
  118.2 2.6 %collective-permute-start.7 = (bf16[128,2048]{1,0:T(8,128)(2,1)S(1)}, bf16[128,2048]{1,0:T(8,128)(2,1)S(1)}, u32[]{:S(2)}, u32[]{:S(2)}) collective-permute-start(bf16[128,2048]{1,0:T(8,128)(2,1)S(1)} %collective-permute-done.4.refs_3_), channel_id=1, source_target_pairs={{0,32},{32,0},{64,96},{96,64},{128,160},{160,128},{192,224},{224,1... | collective-permute-start | bytes 1572872 | tf_op jit(solution)/shard_map/ppermute | solution.py:129
  120.9 0.0 collective-permute-done.5.refs_4_
  120.9 0.0 collective-permute-done.6.refs_5_
  120.9 1.3 collective-permute-done.7.refs_6_
  122.2 6.7 %newton.1 = bf16[32,2048]{1,0:T(8,128)(2,1)S(1)} custom-call(s32[1]{0:T(128)} %bitcast.refs_0_, bf16[128,2048]{1,0:T(8,128)(2,1)S(1)} %all_gather.3.refs_1_, bf16[128,2048]{1,0:T(8,128)(2,1)S(1)} %collective-permute-done.3.refs_2_, bf16[128,2048]{1,0:T(8,128)(2,1)S(1)} %collective-permute-done.4.refs_3_, ...), custom_call_target="tpu_custom_call" | custom-call | tf_op jit(solution)/shard_map/newton/pallas_call | solution.py:175
  128.9 17.5 %all_to_all.11 = bf16[32,16,128]{2,1,0:T(8,128)(2,1)S(1)} all-to-all(bf16[32,16,128]{2,1,0:T(8,128)(2,1)S(1)} %bitcast.28), channel_id=1, replica_groups=mesh['rep'=24,'fsdp'=32] {'fsdp'}, dimensions={0} | all-to-all | bytes 262144 | tf_op jit(solution)/shard_map/all_to_all | solution.py:205
  146.4 0.9 fusion
  (1 shorter events, 0.0 us)
Async XLA Ops:
  4.4 31.6 %copy-start.1 = (s32[32]{0:T(128)S(1)}, s32[32]{0:T(128)}, u32[]{:S(2)}) copy-start(s32[32]{0:T(128)} %owner_ref.1) | copy-start | bytes 388
  4.4 5.3 %collective-permute-start = (bf16[4,3,32,2048]{3,2,1,0:T(8,128)(2,1)S(1)}, bf16[4,3,32,2048]{3,2,1,0:T(8,128)(2,1)S(1)}, u32[]{:S(2)}, u32[]{:S(2)}) collective-permute-start(bf16[4,3,32,2048]{3,2,1,0:T(8,128)(2,1)S(1)} %dynamic-slice_bitcast_fusion), channel_id=1, source_target_pairs={{0,32},{32,0},{64,96},{96,64},{128,160},{160,128},{192,224},{224,1... | collective-permute-start | bytes 4718600 | tf_op jit(solution)/shard_map/ppermute | solution.py:89
  9.9 23.2 %collective-permute-start.1 = (bf16[4,32,2048]{2,1,0:T(8,128)(2,1)S(1)}, bf16[4,32,2048]{2,1,0:T(8,128)(2,1)S(1)}, u32[]{:S(2)}, u32[]{:S(2)}) collective-permute-start(bf16[4,32,2048]{2,1,0:T(8,128)(2,1)S(1)} %get-tuple-element.6), channel_id=1, source_target_pairs={{0,64},{32,736},{64,128},{96,32},{128,192},{160,96},{192,256},{224... | collective-permute-start | bytes 1572872 | tf_op jit(solution)/shard_map/ppermute | solution.py:99
  14.2 66.9 %copy-start = (f32[1,32,1,2048]{3,2,1,0:T(1,128)S(1)}, f32[1,32,1,2048]{3,2,1,0:T(1,128)}, u32[]{:S(2)}) copy-start(f32[1,32,1,2048]{3,2,1,0:T(1,128)} %param.4) | copy-start | bytes 786436
  14.2 21.8 %collective-permute-start.2 = (bf16[4,32,2048]{2,1,0:T(8,128)(2,1)S(1)}, bf16[4,32,2048]{2,1,0:T(8,128)(2,1)S(1)}, u32[]{:S(2)}, u32[]{:S(2)}) collective-permute-start(bf16[4,32,2048]{2,1,0:T(8,128)(2,1)S(1)} %get-tuple-element.7), channel_id=1, source_target_pairs={{0,704},{32,96},{64,0},{96,160},{128,64},{160,224},{192,128},{224,... | collective-permute-start | bytes 1572872 | tf_op jit(solution)/shard_map/ppermute | solution.py:99
  101.5 14.8 %collective-permute-start.3 = (bf16[128,2048]{1,0:T(8,128)(2,1)S(1)}, bf16[128,2048]{1,0:T(8,128)(2,1)S(1)}, u32[]{:S(2)}, u32[]{:S(2)}) collective-permute-start(bf16[128,2048]{1,0:T(8,128)(2,1)S(1)} %all_gather.3.refs_1_), channel_id=1, source_target_pairs={{0,64},{32,96},{64,128},{96,160},{128,192},{160,224},{192,256},{22... | collective-permute-start | bytes 1572872 | tf_op jit(solution)/shard_map/ppermute | solution.py:128
  105.3 13.0 %collective-permute-start.4 = (bf16[128,2048]{1,0:T(8,128)(2,1)S(1)}, bf16[128,2048]{1,0:T(8,128)(2,1)S(1)}, u32[]{:S(2)}, u32[]{:S(2)}) collective-permute-start(bf16[128,2048]{1,0:T(8,128)(2,1)S(1)} %all_gather.3.refs_1_), channel_id=1, source_target_pairs={{0,704},{32,736},{64,0},{96,32},{128,64},{160,96},{192,128},{224,1... | collective-permute-start | bytes 1572872 | tf_op jit(solution)/shard_map/ppermute | solution.py:128
  108.5 12.3 %collective-permute-start.5 = (bf16[128,2048]{1,0:T(8,128)(2,1)S(1)}, bf16[128,2048]{1,0:T(8,128)(2,1)S(1)}, u32[]{:S(2)}, u32[]{:S(2)}) collective-permute-start(bf16[128,2048]{1,0:T(8,128)(2,1)S(1)} %all_gather.3.refs_1_), channel_id=1, source_target_pairs={{0,32},{32,0},{64,96},{96,64},{128,160},{160,128},{192,224},{224,1... | collective-permute-start | bytes 1572872 | tf_op jit(solution)/shard_map/ppermute | solution.py:129
  116.3 4.6 %collective-permute-start.6 = (bf16[128,2048]{1,0:T(8,128)(2,1)S(1)}, bf16[128,2048]{1,0:T(8,128)(2,1)S(1)}, u32[]{:S(2)}, u32[]{:S(2)}) collective-permute-start(bf16[128,2048]{1,0:T(8,128)(2,1)S(1)} %collective-permute-done.3.refs_2_), channel_id=1, source_target_pairs={{0,32},{32,0},{64,96},{96,64},{128,160},{160,128},{192,224},{224,1... | collective-permute-start | bytes 1572872 | tf_op jit(solution)/shard_map/ppermute | solution.py:129
  118.2 3.9 %collective-permute-start.7 = (bf16[128,2048]{1,0:T(8,128)(2,1)S(1)}, bf16[128,2048]{1,0:T(8,128)(2,1)S(1)}, u32[]{:S(2)}, u32[]{:S(2)}) collective-permute-start(bf16[128,2048]{1,0:T(8,128)(2,1)S(1)} %collective-permute-done.4.refs_3_), channel_id=1, source_target_pairs={{0,32},{32,0},{64,96},{96,64},{128,160},{160,128},{192,224},{224,1... | collective-permute-start | bytes 1572872 | tf_op jit(solution)/shard_map/ppermute | solution.py:129
